TPU v7x, 128 devices: a whole 4x4x4 slice. The times are simulated.
128 devices in a mesh: dom: 16 (over z, x), band: 8 (over y, core).
Axes of the slice: x: 4, y: 4, z: 4, core: 2. Of those that a mesh axis runs over, the one named last changes fastest.
Arguments:
- states: float32 [320, 96, 3584], P('band', 'dom'), may hold values from -6 to 6
- potential: float32 [96, 3584], P('dom'), may hold values from -4 to 1
- counts: int32 [8], replicated, may hold values from 1 to 40, 256 in all
Outputs:
- filtered: float32 [320, 96, 3584], P('band', 'dom')
- projected: float32 [2, 320, 320], P(None, 'band', 'dom')
Inputs may be any that keep to these rules, and one draw needn't show every extreme that they name: The counts sum to 256; the largest equals 40.
All inputs are finite; a program needn't handle non-finite values.
Results may differ from a plain program's by a relative error of at most 0.000057.
Values sent between devices are 32-bit elements; how exact they have to be, the bound alone decides.
No kernel may reach another device: no remote copies, remote signals or barrier semaphores. Data moves between devices by JAX's collectives and lax.ppermute only.
A program may use at most 128 MiB of HBM per device.

v0:
```python
import math

import jax
import jax.numpy as jnp
from jax import lax
from jax.sharding import PartitionSpec as P

NY = 56
NZ = 64


def padded_2(block, sides, width):
    for axis, dim in sides:
        count = lax.axis_size(axis)
        forward = [(i, i + 1) for i in range(count - 1)]
        backward = [(target, source) for source, target in forward]
        low = lax.ppermute(
            lax.slice_in_dim(block, block.shape[dim] - width, None, axis=dim), axis, forward
        )
        high = lax.ppermute(lax.slice_in_dim(block, 0, width, axis=dim), axis, backward)
        block = jnp.concatenate([low, block, high], axis=dim)
    return block


def stencil_weights():
    fact = math.factorial
    sides = [
        2.0 * (-1.0) ** (k + 1) * fact(6) ** 2 / (k * k * fact(6 - k) * fact(6 + k))
        for k in range(1, 7)
    ]
    return (-2.0 * sum(sides), sides)


def apply_hamiltonian(field, potential):
    center_weight, side_weights = stencil_weights()
    span_x, span_y, span_z = (field.shape[1], field.shape[2], field.shape[3])
    extended = padded_2(field, (("dom", 1),), 6)
    padded = jnp.pad(field, ((0, 0), (0, 0), (6, 6), (6, 6)))
    total = 3.0 * center_weight * field
    for step in range(1, 7):
        factor = side_weights[step - 1]
        near = extended[:, 6 + step : 6 + step + span_x]
        near = near + extended[:, 6 - step : 6 - step + span_x]
        near = near + padded[:, :, 6 + step : 6 + step + span_y, 6 : 6 + span_z]
        near = near + padded[:, :, 6 - step : 6 - step + span_y, 6 : 6 + span_z]
        near = near + padded[:, :, 6 : 6 + span_y, 6 + step : 6 + step + span_z]
        near = near + padded[:, :, 6 : 6 + span_y, 6 - step : 6 - step + span_z]
        total = total + factor * near
    return potential[None] * field - 0.5 * (1.0 / 0.36) * total


def contract_cells(left, right):
    return lax.dot_general(
        left,
        right,
        (((1,), (1,)), ((), ())),
        precision=lax.Precision.HIGHEST,
        preferred_element_type=jnp.float32,
    )


def local(states, potential, counts):
    capacity = states.shape[0]
    planes = states.shape[1]
    grid_states = states.reshape(capacity, planes, NY, NZ)
    grid_potential = potential.reshape(planes, NY, NZ)
    live_count = counts[lax.axis_index("band")]
    keep = (jnp.arange(capacity, dtype=jnp.int32) < live_count).astype(jnp.float32)
    start = grid_states * keep[:, None, None, None]
    first = (apply_hamiltonian(start, grid_potential) - 11.0 * start) / 11.0
    second = 2.0 * (apply_hamiltonian(first, grid_potential) - 11.0 * first) / 11.0 - start
    filtered = 2.0 * (apply_hamiltonian(second, grid_potential) - 11.0 * second) / 11.0 - first
    image = apply_hamiltonian(filtered, grid_potential)
    flat_states = filtered.reshape(capacity, -1)
    flat_image = image.reshape(capacity, -1)
    piece = lax.all_gather(flat_states, "band", axis=0, tiled=True)
    terms = jnp.stack([contract_cells(flat_states, piece), contract_cells(flat_image, piece)])
    projected = lax.psum_scatter(terms, "dom", scatter_dimension=2, tiled=True)
    return (filtered.reshape(capacity, planes, NY * NZ), projected)


def solution(mesh):
    return jax.shard_map(
        local,
        mesh=mesh,
        in_specs=(P("band", "dom", None), P("dom", None), P()),
        out_specs=(P("band", "dom", None), P(None, "band", "dom")),
        check_vma=False,
    )
```

profile of v0, /device:TPU:0, one launch (start us, length us, event | category | flops | bytes accessed | tf_op | source)
XLA Modules:
  0.0 1335.5 jit_solution(9797648964110626821)
XLA Ops:
  7.2 5.8 reshape.22
  13.6 0.6 compare_convert_fusion
  14.3 6.4 copy_multiply_fusion
  20.7 1.3 collective-permute-start
  22.0 7.3 collective-permute-start.1
  29.4 143.3 %collective-permute-done = f32[40,6,56,64]{3,2,1,0:T(8,128)} collective-permute-done((f32[40,6,56,64]{3,2,1,0:T(8,128)}, f32[40,6,56,64]{3,2,1,0:T(8,128)}, u32[]{:S(2)}, u32[]{:S(2)}) %collective-permute-start) | collective-permute-done | bytes 3440672 | tf_op jit(solution)/shard_map/ppermute | solution.py:20
  172.7 1.2 collective-permute-done.1
  173.9 134.6 %broadcast_multiply_fusion = (f32[40,6,56,64]{3,2,1,0:T(8,128)}, f32[40,6,56,64]{3,2,1,0:T(8,128)}) fusion(f32[40,6,56,64]{3,2,1,0:T(8,128)} %copy_multiply_fusion, f32[40,6,56,64]{3,2,1,0:T(8,128)} %collective-permute-done, f32[40,6,56,64]{3,2,1,0:T(8,128)} %collective-permute-done.1, f32[6,56,64]{2,1,0:T(8,128)S(1)} %mul.149), kind=kLoop, calls=%fused_computation.380 | loop fusion | flops 50749440 | bytes 17289216 | tf_op jit(solution)/shard_map/div | solution.py:70
  308.5 7.3 collective-permute-start.3
  315.7 1.3 collective-permute-start.2
  317.0 142.3 %collective-permute-done.3 = f32[40,6,56,64]{3,2,1,0:T(8,128)} collective-permute-done((f32[40,6,56,64]{3,2,1,0:T(8,128)}, f32[40,6,56,64]{3,2,1,0:T(8,128)}, u32[]{:S(2)}, u32[]{:S(2)}) %collective-permute-start.3) | collective-permute-done | bytes 3440672 | tf_op jit(solution)/shard_map/ppermute | solution.py:17
  459.3 7.0 collective-permute-done.2
  466.3 133.7 %fusion.54 = f32[40,6,56,64]{3,2,1,0:T(8,128)} fusion(f32[40,6,56,64]{3,2,1,0:T(8,128)} %get-tuple-element.7, f32[40,6,56,64]{3,2,1,0:T(8,128)} %get-tuple-element.6, f32[40,6,56,64]{3,2,1,0:T(8,128)} %collective-permute-done.3, f32[40,6,56,64]{3,2,1,0:T(8,128)} %collective-permute-done.2, f32[6,56,64]{2,1,0:T(8,128)S(1)} %broadcast_multiply_fusion.1, ...), kind=kLoop, calls=%fused_computation.214 | loop fusion | flops 51609600 | bytes 20730016 | tf_op jit(solution)/shard_map/sub | solution.py:71
  600.0 1.9 collective-permute-start.5
  601.9 1.5 collective-permute-start.4
  603.5 143.7 %collective-permute-done.5 = f32[40,6,56,64]{3,2,1,0:T(8,128)S(1)} collective-permute-done((f32[40,6,56,64]{3,2,1,0:T(8,128)}, f32[40,6,56,64]{3,2,1,0:T(8,128)S(1)}, u32[]{:S(2)}, u32[]{:S(2)}) %collective-permute-start.5) | collective-permute-done | bytes 3440672 | tf_op jit(solution)/shard_map/ppermute | solution.py:17
  747.2 7.0 collective-permute-done.4
  754.2 130.1 %fusion.95 = f32[40,6,56,64]{3,2,1,0:T(8,128)} fusion(f32[40,6,56,64]{3,2,1,0:T(8,128)} %fusion.54, f32[40,6,56,64]{3,2,1,0:T(8,128)S(1)} %collective-permute-done.5, f32[40,6,56,64]{3,2,1,0:T(8,128)} %collective-permute-done.4, f32[40,6,56,64]{3,2,1,0:T(8,128)} %get-tuple-element.7, f32[6,56,64]{2,1,0:T(8,128)S(1)} %mul.149), kind=kLoop, calls=%fused_computation.255 | loop fusion | flops 52469760 | bytes 17289216 | tf_op jit(solution)/shard_map/sub | solution.py:72
  884.2 5.8 reshape.24
  890.1 5.9 collective-permute-start.7
  896.0 1.3 collective-permute-start.6
  897.3 142.8 %collective-permute-done.7 = f32[40,6,56,64]{3,2,1,0:T(8,128)S(1)} collective-permute-done((f32[40,6,56,64]{3,2,1,0:T(8,128)}, f32[40,6,56,64]{3,2,1,0:T(8,128)S(1)}, u32[]{:S(2)}, u32[]{:S(2)}) %collective-permute-start.7) | collective-permute-done | bytes 3440672 | tf_op jit(solution)/shard_map/ppermute | solution.py:17
  1040.2 4.6 collective-permute-done.6
  1044.7 128.0 %fusion.133 = f32[40,6,56,64]{3,2,1,0:T(8,128)} fusion(f32[40,6,56,64]{3,2,1,0:T(8,128)} %fusion.95, f32[40,6,56,64]{3,2,1,0:T(8,128)S(1)} %collective-permute-done.7, f32[40,6,56,64]{3,2,1,0:T(8,128)} %collective-permute-done.6, f32[6,56,64]{2,1,0:T(8,128)S(1)} %mul.149), kind=kLoop, calls=%fused_computation.293 | loop fusion | flops 48168960 | bytes 13848576 | tf_op jit(solution)/shard_map/sub | solution.py:49
  1172.7 6.0 reshape.25
  1178.7 26.0 %convolution_bitcast_fusion.1 = f32[1,40,320]{2,1,0:T(8,128)S(1)} fusion(f32[40,21504]{1,0:T(8,128)S(1)} %copy-done.1, f32[320,21504]{1,0:T(8,128)} %all-gather.2.cloned.1.call-done), kind=kOutput, calls=%fused_computation.382 | convolution fusion | flops 3303014400 | bytes 31016960 | tf_op jit(solution)/shard_map/dot_general | solution.py:53
  1204.8 33.3 %convolution_bitcast_fusion = f32[1,40,320]{2,1,0:T(8,128)S(1)} fusion(f32[40,21504]{1,0:T(8,128)} %reshape.25, f32[320,21504]{1,0:T(8,128)S(1)} %copy-done), kind=kOutput, calls=%fused_computation.381 | convolution fusion | flops 3303014400 | bytes 31016960 | tf_op jit(solution)/shard_map/dot_general | solution.py:53
  1238.1 0.9 copy.11
  1240.3 7.4 reshape.26
  1247.7 6.1 copy.12
  1253.7 73.4 %all-reduce.7.cloned.1.call-done = f32[2,40,320]{1,0,2:T(2,128)} async-done(((f32[2,40,320]{1,0,2:T(2,128)}), f32[2,40,320]{1,0,2:T(2,128)}) %all-reduce.7.cloned.1.call-update) | async-done | bytes 102416
  1327.1 1.3 constant_dynamic-slice_fusion
  (25 shorter events, 1.4 us)
Async XLA Ops:
  7.2 5.9 copy-start.3
  7.2 1171.5 %all-gather.2.cloned.1.call-start = ((), (), s32[]{:S(2)}) async-start(), calls=%async_computation | async-start | bytes 30965760 | tf_op jit(solution)/shard_map/all_gather | solution.py:76
  14.3 15.0 %copy-start.2 = (f32[6,3584]{1,0:T(8,128)S(1)}, f32[6,3584]{1,0:T(8,128)}, u32[]{:S(2)}) copy-start(f32[6,3584]{1,0:T(8,128)} %param.4) | copy-start | bytes 258052
  20.7 152.0 %collective-permute-start = (f32[40,6,56,64]{3,2,1,0:T(8,128)}, f32[40,6,56,64]{3,2,1,0:T(8,128)}, u32[]{:S(2)}, u32[]{:S(2)}) collective-permute-start(f32[40,6,56,64]{3,2,1,0:T(8,128)} %copy_multiply_fusion), channel_id=1, source_target_pairs={{8,0},{16,8},{24,16},{32,24},{40,32},{48,40},{56,48},{64,56},{72,6... | collective-permute-start | bytes 10321928 | tf_op jit(solution)/shard_map/ppermute | solution.py:20
  22.0 151.9 %collective-permute-start.1 = (f32[40,6,56,64]{3,2,1,0:T(8,128)}, f32[40,6,56,64]{3,2,1,0:T(8,128)}, u32[]{:S(2)}, u32[]{:S(2)}) collective-permute-start(f32[40,6,56,64]{3,2,1,0:T(8,128)} %copy_multiply_fusion), channel_id=1, source_target_pairs={{0,8},{8,16},{16,24},{24,32},{32,40},{40,48},{48,56},{56,64},{64,7... | collective-permute-start | bytes 10321928 | tf_op jit(solution)/shard_map/ppermute | solution.py:17
  29.3 437.0 %slice-start = ((s8[6881280]{0:T(1024)(128)(4,1)}), s8[2686976]{0:T(1024)(128)(4,1)S(1)}, s32[]{:S(2)}) async-start(s8[6881280]{0:T(1024)(128)(4,1)} %bitcast.18), calls=%async_computation.2 | async-start | bytes 5373952
  29.4 436.9 %slice-start.1 = ((s8[6881280]{0:T(1024)(128)(4,1)}), s8[4194304]{0:T(1024)(128)(4,1)S(1)}, s32[]{:S(2)}) async-start(s8[6881280]{0:T(1024)(128)(4,1)} %bitcast.18), calls=%async_computation.3 | async-start | bytes 8388608
  308.5 150.8 %collective-permute-start.3 = (f32[40,6,56,64]{3,2,1,0:T(8,128)}, f32[40,6,56,64]{3,2,1,0:T(8,128)}, u32[]{:S(2)}, u32[]{:S(2)}) collective-permute-start(f32[40,6,56,64]{3,2,1,0:T(8,128)} %get-tuple-element.6), channel_id=1, source_target_pairs={{0,8},{8,16},{16,24},{24,32},{32,40},{40,48},{48,56},{56,64},{64,7... | collective-permute-start | bytes 10321928 | tf_op jit(solution)/shard_map/ppermute | solution.py:17
  315.7 150.5 %collective-permute-start.2 = (f32[40,6,56,64]{3,2,1,0:T(8,128)}, f32[40,6,56,64]{3,2,1,0:T(8,128)}, u32[]{:S(2)}, u32[]{:S(2)}) collective-permute-start(f32[40,6,56,64]{3,2,1,0:T(8,128)} %get-tuple-element.6), channel_id=1, source_target_pairs={{8,0},{16,8},{24,16},{32,24},{40,32},{48,40},{56,48},{64,56},{72,6... | collective-permute-start | bytes 10321928 | tf_op jit(solution)/shard_map/ppermute | solution.py:20
  600.0 147.2 %collective-permute-start.5 = (f32[40,6,56,64]{3,2,1,0:T(8,128)}, f32[40,6,56,64]{3,2,1,0:T(8,128)S(1)}, u32[]{:S(2)}, u32[]{:S(2)}) collective-permute-start(f32[40,6,56,64]{3,2,1,0:T(8,128)} %fusion.54), channel_id=1, source_target_pairs={{0,8},{8,16},{16,24},{24,32},{32,40},{40,48},{48,56},{56,64},{64,7... | collective-permute-start | bytes 10321928 | tf_op jit(solution)/shard_map/ppermute | solution.py:17
  601.9 152.3 %collective-permute-start.4 = (f32[40,6,56,64]{3,2,1,0:T(8,128)}, f32[40,6,56,64]{3,2,1,0:T(8,128)}, u32[]{:S(2)}, u32[]{:S(2)}) collective-permute-start(f32[40,6,56,64]{3,2,1,0:T(8,128)} %fusion.54), channel_id=1, source_target_pairs={{8,0},{16,8},{24,16},{32,24},{40,32},{48,40},{56,48},{64,56},{72,6... | collective-permute-start | bytes 10321928 | tf_op jit(solution)/shard_map/ppermute | solution.py:20
  890.1 437.0 %all-reduce.7.cloned.1.call-start = ((), (), s32[]{:S(2)}) async-start(), calls=%async_computation.1 | async-start | bytes 655360
  890.1 150.1 %collective-permute-start.7 = (f32[40,6,56,64]{3,2,1,0:T(8,128)}, f32[40,6,56,64]{3,2,1,0:T(8,128)S(1)}, u32[]{:S(2)}, u32[]{:S(2)}) collective-permute-start(f32[40,6,56,64]{3,2,1,0:T(8,128)} %fusion.95), channel_id=1, source_target_pairs={{0,8},{8,16},{16,24},{24,32},{32,40},{40,48},{48,56},{56,64},{64,7... | collective-permute-start | bytes 10321928 | tf_op jit(solution)/shard_map/ppermute | solution.py:17
  896.0 148.7 %collective-permute-start.6 = (f32[40,6,56,64]{3,2,1,0:T(8,128)}, f32[40,6,56,64]{3,2,1,0:T(8,128)}, u32[]{:S(2)}, u32[]{:S(2)}) collective-permute-start(f32[40,6,56,64]{3,2,1,0:T(8,128)} %fusion.95), channel_id=1, source_target_pairs={{8,0},{16,8},{24,16},{32,24},{40,32},{48,40},{56,48},{64,56},{72,6... | collective-permute-start | bytes 10321928 | tf_op jit(solution)/shard_map/ppermute | solution.py:20
  1172.7 6.0 copy-start.1
  1178.7 26.1 %copy-start = (f32[320,21504]{1,0:T(8,128)S(1)}, f32[320,21504]{1,0:T(8,128)}, u32[]{:S(2)}) copy-start(f32[320,21504]{1,0:T(8,128)} %all-gather.2.cloned.1.call-done) | copy-start | bytes 82575360
  1204.8 34.3 %copy-start.4 = (u32[128]{0:T(128)S(1)}, u32[128]{0:T(128)}, u32[]{:S(2)}) copy-start(u32[128]{0:T(128)} %constant.51) | copy-start | bytes 1540
Sparse Core Ops, SparseCore 0:
  890.2 135.6 all-gather.1
  1239.1 87.9 all-reduce.6
where the time goes:
time: 1340 us
  waiting for transfers between devices  665 us (50%)
  other arithmetic  533 us (40%)
  matrix products  59.4 us (4%)
  local copies, waits for them, and re-layouts  34.6 us (3%)
  starting transfers between devices  27.9 us (2%)
  between operations  15 us (1%)
    ppermute x4, waiting for transfers between devices, padded_2(): lax.ppermute(lax.slice_in_dim(block, block.shape[dim] - width, None, axis...  430 us
    ppermute x4, waiting for transfers between devices, padded_2(): lax.ppermute(lax.slice_in_dim(block, 0, width, axis=dim), axis, backward)  162 us
    div x1, other arithmetic, local(): first = (apply_hamiltonian(start, grid_potential) - 11.0 * start) / 11.0  135 us
    sub x1, other arithmetic, local(): 2.0 * (apply_hamiltonian(first, grid_potential) - 11.0 * first) / 11.0  134 us
    sub x1, other arithmetic, local(): 2.0 * (apply_hamiltonian(second, grid_potential) - 11.0 * second) / 11.0  130 us
    sub x1, other arithmetic, apply_hamiltonian(): return potential[None] * field - 0.5 * (1.0 / 0.36) * total  128 us
    unnamed x3, waiting for transfers between devices  73.4 us
    dot_general x2, matrix products, contract_cells(): lax.dot_general(left, right, (((1,), (1,)), ((), ())), precision=lax.Prec...  59.4 us
  transfers between devices with their start and end apart: 10, of which 9 were waited for; matrix products, arithmetic and copies ran while one was open for 11% of the time, Pallas kernels for 0%

commit v1 on v0

v1 whole, which is shorter than its diff:
```python
import math

import jax
import jax.numpy as jnp
import ml_dtypes
import numpy as np
from jax import lax
from jax.experimental import pallas as pl
from jax.experimental.pallas import tpu as pltpu
from jax.sharding import PartitionSpec as P

NY = 56
NZ = 64
NX = 96
CELLS = NY * NZ
TILES = CELLS // 128
CAP = 40
PLANES = 6
EDGE = 384
WIDE = CELLS + 2 * EDGE
ROWS = PLANES * TILES
VMEM = 60 * 1024 * 1024
F32 = jnp.float32
BF16 = jnp.bfloat16


def stencil_weights():
    fact = math.factorial
    sides = [
        2.0 * (-1.0) ** (k + 1) * fact(6) ** 2 / (k * k * fact(6 - k) * fact(6 + k))
        for k in range(1, 7)
    ]
    return (-2.0 * sum(sides), sides)


CENTER, SIDES = stencil_weights()
KINETIC = -0.5 * (1.0 / 0.36)
STEP = [KINETIC * s for s in SIDES]


def halves(matrix):
    exact = matrix.astype(np.float32)
    high = exact.astype(ml_dtypes.bfloat16)
    low = (exact - high.astype(np.float32)).astype(ml_dtypes.bfloat16)
    return high, low


def band_matrix(size):
    out = np.zeros((size, size))
    for k in range(1, 7):
        for i in range(size - k):
            out[i, i + k] = out[i + k, i] = STEP[k - 1]
    return out


def stencil_operands():
    zh, zl = halves(np.kron(np.eye(4), band_matrix(NZ)))
    xh, xl = halves(band_matrix(NX))
    return np.concatenate([zh, zh, zl], axis=0), np.concatenate([xh, xh, xl], axis=1)


def cost(flops, nbytes):
    return pl.CostEstimate(flops=flops, transcendentals=0, bytes_accessed=nbytes)


def params():
    return pltpu.CompilerParams(vmem_limit_bytes=VMEM)


SMEM_SPEC = pl.BlockSpec(memory_space=pltpu.SMEM)


def pack_body(info, states, pot, out0, out1, out2, flat):
    live = info[0]
    lanes = lax.broadcasted_iota(jnp.int32, (8, 128), 0)
    for r in range(TILES):
        flat[pl.ds(r, PLANES, stride=TILES), :] = pot[:, r * 128 : (r + 1) * 128]
    for p in range(PLANES):
        piece = flat[p * TILES : (p + 1) * TILES, :]
        for d in range(16):
            base = (d * PLANES + p) * 2 * TILES + TILES
            out0[base : base + TILES, :] = piece

    def plane(p, carry):
        for i in range(5):
            keep = (lanes + 8 * i) < live
            for r in range(TILES):
                v = states[p, 8 * i : 8 * i + 8, r * 128 : (r + 1) * 128]
                v = jnp.where(keep, v, 0.0)
                if i < 2:
                    out0[pl.ds(8 * i * 2 * ROWS + p * 2 * TILES + r, 8, stride=2 * ROWS), :] = v
                elif i < 4:
                    out1[pl.ds(8 * (i - 2) * ROWS + p * TILES + r, 8, stride=ROWS), :] = v
                else:
                    for q in range(2):
                        out2[pl.ds(8 * q * ROWS + p * TILES + r, 8, stride=ROWS), :] = v
        return carry

    lax.fori_loop(0, PLANES, plane, 0)


def pack(info, states, pot):
    return pl.pallas_call(
        pack_body,
        out_shape=(
            jax.ShapeDtypeStruct((16 * 2 * ROWS, 128), F32),
            jax.ShapeDtypeStruct((16 * ROWS, 128), F32),
            jax.ShapeDtypeStruct((16 * ROWS, 128), F32),
        ),
        in_specs=[SMEM_SPEC, pl.BlockSpec(), pl.BlockSpec()],
        scratch_shapes=[pltpu.VMEM((ROWS, 128), F32)],
        compiler_params=params(),
        cost_estimate=cost(4_000_000, 10_000_000),
        name="pack",
    )(info, states, pot)


def split(value):
    high = value.astype(BF16)
    return high, (value - high.astype(F32)).astype(BF16)


def comp_body(first, half, *refs):
    if first:
        recv, wz, ax, out, diag = refs[:5]
        refs = refs[5:]
    elif half:
        info, recv, diag, wz, ax, out = refs[:6]
        refs = refs[6:]
    else:
        recv, diag, wz, ax, out = refs[:5]
        refs = refs[5:]
    va, vb, ua, ub, ha, hb, la, lb = refs
    stride = 2 * TILES if first else TILES
    zero = jnp.zeros((NX, EDGE), F32)
    for ref in (va, vb, ua, ub):
        ref[:, :EDGE] = zero
        ref[:, EDGE + CELLS :] = zero

    def load(r, carry):
        at = pl.multiple_of(r * 128, 128)
        tiles = [recv[pl.ds(8 * i * stride + r, 8, stride=stride), :] for i in range(12)]
        v = jnp.concatenate(tiles, axis=0)
        va[:, pl.ds(EDGE + at, 128)] = v
        ua[:, pl.ds(EDGE + at, 128)] = pltpu.roll(v, 64, 1)
        high, low = split(v)
        ha[:, pl.ds(at, 128)] = high
        la[:, pl.ds(at, 128)] = low
        if first:
            tiles = [
                recv[pl.ds(8 * i * stride + TILES + r, 8, stride=stride), :] for i in range(12)
            ]
            diag[:, pl.ds(at, 128)] = jnp.concatenate(tiles, axis=0) + KINETIC * 3.0 * CENTER
        return carry

    lax.fori_loop(0, TILES, load, 0)
    low_half = (lax.broadcasted_iota(jnp.int32, (NX, 256), 1) % 128) < 64

    def apply(src, dst, stage):
        v_src, u_src, h_src, l_src = src
        v_dst, u_dst, h_dst, l_dst = dst

        def block(cb, carry):
            at = pl.multiple_of(cb * 256, 256)

            def v_at(k):
                return v_src[:, pl.ds(EDGE + at + 128 * k, 256)]

            def u_at(k):
                return u_src[:, pl.ds(EDGE + at + 128 * k, 384)]

            h = h_src[:, pl.ds(at, 256)]
            l = l_src[:, pl.ds(at, 256)]
            acc = jnp.dot(
                jnp.concatenate([h, l, h], axis=1), wz[...], preferred_element_type=F32
            )
            acc = acc + jnp.dot(
                ax[...], jnp.concatenate([h, l, h], axis=0), preferred_element_type=F32
            )
            odd = STEP[0] * (u_at(0) + u_at(-1))
            odd = odd + STEP[2] * (u_at(1) + u_at(-2))
            odd = odd + STEP[4] * (u_at(2) + u_at(-3))
            acc = acc + jnp.where(low_half, odd[:, :256], odd[:, 128:])
            acc = acc + STEP[1] * (v_at(1) + v_at(-1))
            acc = acc + STEP[3] * (v_at(2) + v_at(-2))
            acc = acc + STEP[5] * (v_at(3) + v_at(-3))
            v = v_at(0)
            new = acc + diag[:, pl.ds(at, 256)] * v
            if stage == 1:
                new = new * (1.0 / 11.0) - v
            elif stage < 4:
                new = new * (2.0 / 11.0) - 2.0 * v - v_dst[:, pl.ds(EDGE + at, 256)]
            v_dst[:, pl.ds(EDGE + at, 256)] = new
            if stage < 4:
                for j in range(2):
                    u_dst[:, pl.ds(EDGE + at + 128 * j, 128)] = pltpu.roll(
                        new[:, 128 * j : 128 * j + 128], 64, 1
                    )
                high, low = split(new)
                h_dst[:, pl.ds(at, 256)] = high
                l_dst[:, pl.ds(at, 256)] = low
            return carry

        lax.fori_loop(0, CELLS // 256, block, 0)

    a, b = (va, ua, ha, la), (vb, ub, hb, lb)
    apply(a, b, 1)
    apply(b, a, 2)
    apply(a, b, 3)
    apply(b, a, 4)
    count = TILES // 2 if half else TILES
    begin = info[1] * (count * 128) if half else 0

    def store(r, carry):
        at = pl.multiple_of(EDGE + begin + r * 128, 128)
        for which, ref in ((0, vb), (1, va)):
            for i in range(12):
                out[pl.ds(8 * i * 2 * count + which * count + r, 8, stride=2 * count), :] = ref[
                    8 * i : 8 * i + 8, pl.ds(at, 128)
                ]
        return carry

    lax.fori_loop(0, count, store, 0)


def comp(first, half, args, name):
    rows = NX * TILES * (1 if half else 2)
    out_shape = [jax.ShapeDtypeStruct((rows, 128), F32)]
    if first:
        out_shape.append(jax.ShapeDtypeStruct((NX, CELLS), F32))
    wide = pltpu.VMEM((NX, WIDE), F32)
    narrow = pltpu.VMEM((NX, CELLS), BF16)
    in_specs = [pl.BlockSpec()] * len(args)
    if half:
        in_specs[0] = SMEM_SPEC

    def body(*refs):
        comp_body(first, half, *refs)

    return pl.pallas_call(
        body,
        out_shape=tuple(out_shape),
        in_specs=in_specs,
        scratch_shapes=[wide] * 4 + [narrow] * 4,
        compiler_params=params(),
        cost_estimate=cost(15_000_000_000, 10_000_000),
        name=name,
    )(*args)


def unpack_body(recv0, recv1, recv2, filtered, send_f, send_i):
    for p in range(PLANES):
        for r in range(TILES):
            b, t = divmod(p * TILES + r, 21)
            for which in range(2):
                send = send_i if which else send_f
                for i in range(5):
                    if i < 4:
                        recv = recv0 if i < 2 else recv1
                        start = 8 * (i % 2) * 2 * ROWS + p * 2 * TILES + which * TILES + r
                        v = recv[pl.ds(start, 8, stride=2 * ROWS), :]
                    else:
                        q, rest = divmod(r, TILES // 2)
                        start = 8 * q * ROWS + p * TILES + which * (TILES // 2) + rest
                        v = recv2[pl.ds(start, 8, stride=ROWS), :]
                    rows = slice(8 * i, 8 * i + 8)
                    send[b, rows, t * 128 : (t + 1) * 128] = v
                    if not which:
                        filtered[p, rows, r * 128 : (r + 1) * 128] = v


def unpack(recv0, recv1, recv2):
    return pl.pallas_call(
        unpack_body,
        out_shape=(
            jax.ShapeDtypeStruct((PLANES, CAP, CELLS), F32),
            jax.ShapeDtypeStruct((8, CAP, 21 * 128), F32),
            jax.ShapeDtypeStruct((8, CAP, 21 * 128), F32),
        ),
        compiler_params=params(),
        cost_estimate=cost(4_000_000, 17_000_000),
        name="unpack",
    )(recv0, recv1, recv2)


KSTEP = 7 * 128


def product(left, right):
    lh, ll = split(left)
    rh, rl = split(right)
    total = None
    for one, two in ((lh, rh), (lh, rl), (ll, rh)):
        term = lax.dot_general(one, two, (((1,), (1,)), ((), ())), preferred_element_type=F32)
        total = term if total is None else total + term
    return total


def overlap_body(left, out):
    term = product(left[...], left[...])

    @pl.when(pl.program_id(0) == 0)
    def _():
        out[...] = term

    @pl.when(pl.program_id(0) > 0)
    def _():
        out[...] += term


def overlap(full):
    n = full.shape[0]
    return pl.pallas_call(
        overlap_body,
        grid=(3,),
        out_shape=jax.ShapeDtypeStruct((n, n), F32),
        in_specs=[pl.BlockSpec((n, KSTEP), lambda k: (0, k))],
        out_specs=pl.BlockSpec((n, n), lambda k: (0, 0)),
        compiler_params=params(),
        cost_estimate=cost(2_000_000_000, 4_000_000),
        name="overlap",
    )(full)


def energy_body(left, right, inter, out, acc):
    term = product(left[...], right[...])

    @pl.when(pl.program_id(0) == 0)
    def _():
        acc[...] = term

    @pl.when(pl.program_id(0) > 0)
    def _():
        acc[...] += term

    @pl.when(pl.program_id(0) == 2)
    def _():
        for d in range(16):
            out[d, :20, :] = inter[20 * d : 20 * d + 20, :]
            out[d, 20:40, :] = acc[20 * d : 20 * d + 20, :]


def energy(full, image, inter):
    n = full.shape[0]
    return pl.pallas_call(
        energy_body,
        grid=(3,),
        out_shape=jax.ShapeDtypeStruct((16, 40, n), F32),
        in_specs=[
            pl.BlockSpec((n, KSTEP), lambda k: (0, k)),
            pl.BlockSpec((n, KSTEP), lambda k: (0, k)),
            pl.BlockSpec((n, n), lambda k: (0, 0)),
        ],
        out_specs=pl.BlockSpec((16, 40, n), lambda k: (0, 0, 0)),
        scratch_shapes=[pltpu.VMEM((n, n), F32)],
        compiler_params=params(),
        cost_estimate=cost(2_000_000_000, 8_000_000),
        name="energy",
    )(full, image, inter)


def exchange(value, axis, parts):
    shape = value.shape
    value = value.reshape((parts, -1) + shape[-1:])
    return lax.all_to_all(value, axis, 0, 0, tiled=True).reshape(shape)


def local(states, potential, counts):
    wz, ax = (jnp.asarray(m) for m in stencil_operands())
    live = counts[lax.axis_index("band")]
    info = jnp.stack([live, lax.axis_index("dom") // 8]).astype(jnp.int32)
    send0, send1, send2 = pack(info, jnp.transpose(states, (1, 0, 2)), potential)
    recv0 = exchange(send0, "dom", 16)
    recv0, send1 = lax.optimization_barrier((recv0, send1))
    recv1 = exchange(send1, "dom", 16)
    out0, diag = comp(True, False, (recv0, wz, ax), "comp0")
    recv1, send2 = lax.optimization_barrier((recv1, send2))
    recv2 = exchange(send2, "dom", 16)
    (out1,) = comp(False, False, (recv1, diag, wz, ax), "comp1")
    recv2, out0 = lax.optimization_barrier((recv2, out0))
    back0 = exchange(out0, "dom", 16)
    (out2,) = comp(False, True, (info, recv2, diag, wz, ax), "comp2")
    back0, out1 = lax.optimization_barrier((back0, out1))
    back1 = exchange(out1, "dom", 16)
    back1, out2 = lax.optimization_barrier((back1, out2))
    back2 = exchange(out2, "dom", 16)
    filtered, send_f, send_i = unpack(back0, back1, back2)
    full = lax.all_to_all(send_f, "band", 0, 0, tiled=True)
    full, send_i = lax.optimization_barrier((full, send_i))
    image = lax.all_to_all(send_i, "band", 0, 0, tiled=True)
    full = full.reshape(8 * CAP, 21 * 128)
    image = image.reshape(8 * CAP, 21 * 128)
    terms = energy(full, image, overlap(full))
    terms = lax.all_to_all(terms, "dom", 0, 0, tiled=True).sum(axis=0)
    terms = jnp.transpose(terms.reshape(2, 20, 8, CAP), (2, 0, 1, 3)).reshape(8, 40, CAP)
    terms = lax.all_to_all(terms, "band", 0, 0, tiled=True).sum(axis=0)
    projected = jnp.transpose(terms.reshape(2, 20, CAP), (0, 2, 1))
    return (jnp.transpose(filtered, (1, 0, 2)), projected)


def solution(mesh):
    return jax.shard_map(
        local,
        mesh=mesh,
        in_specs=(P("band", "dom", None), P("dom", None), P()),
        out_specs=(P("band", "dom", None), P(None, "band", "dom")),
        check_vma=False,
    )
```

time: 1340 us -> 357 us (0.27)
  waiting for transfers between devices: 665 us -> 60.1 us
  other arithmetic: 533 us -> 2.04 us
  blocking collectives: 0 us -> 165 us
  Pallas kernels: 0 us -> 102 us
  matrix products: 59.4 us -> 0 us
  local copies, waits for them, and re-layouts: 34.6 us -> 7.09 us
  between operations: 15 us -> 0.75 us
    ppermute x8 -> x0, waiting for transfers between devices: 592 us -> none  [the longest x4 430 us: padded_2(): lax.ppermute(lax.slice_in_dim(block, block.shape[dim] - width, None, axis...]
    sub x3 -> x0, other arithmetic: 392 us -> none  [the longest x1 134 us: local(): 2.0 * (apply_hamiltonian(first, grid_potential) - 11.0 * first) / 11.0]
    all_to_all x0 -> x6, blocking collectives: none -> 165 us  [the longest x3 90.9 us: exchange(): return lax.all_to_all(value, axis, 0, 0, tiled=True).reshape(shape)]
    div x1 -> x0, other arithmetic: 135 us -> none  [local(): first = (apply_hamiltonian(start, grid_potential) - 11.0 * start) / 11.0]
    pallas_call x0 -> x7, Pallas kernels: none -> 102 us  [the longest x3 76 us: comp(): pl.pallas_call(body, out_shape=tuple(out_shape), in_specs=in_specs, scrat...]
    unnamed x3 -> x0, waiting for transfers between devices: 73.4 us -> none
    all_to_all x0 -> x4, waiting for transfers between devices: none -> 60.1 us  [the longest x1 35.9 us: local(): image = lax.all_to_all(send_i, 'band', 0, 0, tiled=True)]
    dot_general x2 -> x0, matrix products: 59.4 us -> none  [contract_cells(): lax.dot_general(left, right, (((1,), (1,)), ((), ())), precision=lax.Prec...]
  transfers between devices with their start and end apart: 10 -> 4, of which waited for: 9 -> 3; matrix products, arithmetic and copies ran while one was open for 11% -> 0% of each run, Pallas kernels for 0% -> 23%
where the time goes in v1:
time: 357 us; the launch traced here: 356 us
  blocking collectives  165 us (46%)
  Pallas kernels  102 us (29%)
  waiting for transfers between devices  60.1 us (17%)
  starting transfers between devices  19 us (5%)
  local copies, waits for them, and re-layouts  7.09 us (2%)
    all_to_all x3, blocking collectives, exchange(): return lax.all_to_all(value, axis, 0, 0, tiled=True).reshape(shape)  90.9 us
    pallas_call x3, Pallas kernels, comp(): pl.pallas_call(body, out_shape=tuple(out_shape), in_specs=in_specs, scrat...  76 us
    all_to_all x1, blocking collectives, local(): full = lax.all_to_all(send_f, 'band', 0, 0, tiled=True)  46.2 us
    all_to_all x1, waiting for transfers between devices, local(): image = lax.all_to_all(send_i, 'band', 0, 0, tiled=True)  35.9 us
    all_to_all x3, waiting for transfers between devices, exchange(): return lax.all_to_all(value, axis, 0, 0, tiled=True).reshape(shape)  24.2 us
    all_to_all x1, blocking collectives, local(): terms = lax.all_to_all(terms, 'dom', 0, 0, tiled=True).sum(axis=0)  20 us
    all_to_all x3, starting transfers between devices, exchange(): return lax.all_to_all(value, axis, 0, 0, tiled=True).reshape(shape)  15.3 us
    pallas_call x1, Pallas kernels, unpack(): pl.pallas_call(unpack_body, out_shape=(jax.ShapeDtypeStruct((PLANES, CAP,...  7.99 us
  transfers between devices with their start and end apart: 4, of which 3 were waited for; matrix products, arithmetic and copies ran while one was open for 0% of the time, Pallas kernels for 23%

profile of v1, /device:TPU:0, one launch (start us, length us, event | category | flops | bytes accessed | tf_op | source)
XLA Modules:
  0.0 355.7 jit_solution(7371588410438015488)
XLA Ops:
  0.6 1.2 dynamic_slice.3
  1.9 1.2 pad_add_fusion.info.refs_0_
  3.1 5.4 %pack.1 = (f32[5376,128]{1,0:T(8,128)}, f32[2688,128]{1,0:T(8,128)}, f32[2688,128]{1,0:T(8,128)}) custom-call(s32[2]{0:T(128)} %pad_add_fusion.info.refs_0_, f32[6,40,3584]{2,1,0:T(8,128)} %bitcast.26, f32[6,3584]{1,0:T(8,128)} %pot.1), custom_call_target="tpu_custom_call" | custom-call | flops 4000000 | bytes 10000000 | tf_op jit(solution)/shard_map/pack/pallas_call | solution.py:103
  8.5 43.6 %all_to_all.50 = f32[16,336,128]{2,1,0:T(8,128)} all-to-all(f32[16,336,128]{2,1,0:T(8,128)} %bitcast.30), channel_id=1, replica_groups=mesh['dom'=16,'band'=8] {'dom'}, dimensions={0} | all-to-all | bytes 5505024 | tf_op jit(solution)/shard_map/all_to_all | solution.py:365
  52.1 23.1 %all_to_all.51 = f32[16,168,128]{2,1,0:T(8,128)} all-to-all(f32[16,168,128]{2,1,0:T(8,128)S(1)} %bitcast.34), channel_id=1, replica_groups=mesh['dom'=16,'band'=8] {'dom'}, dimensions={0} | all-to-all | bytes 2752512 | tf_op jit(solution)/shard_map/all_to_all | solution.py:365
  75.2 3.7 %all-to-all-start.2 = ((f32[16,168,128]{2,1,0:T(8,128)}), f32[16,168,128]{2,1,0:T(8,128)S(1)}, u32[]{:S(2)}, u32[]{:S(2)}) async-start(f32[16,168,128]{2,1,0:T(8,128)} %bitcast.6), calls=%async_computation.2 | async-start | bytes 2752512 | tf_op jit(solution)/shard_map/all_to_all | solution.py:365
  78.9 26.2 %comp0.1 = (f32[5376,128]{1,0:T(8,128)}, f32[96,3584]{1,0:T(8,128)}) custom-call(f32[5376,128]{1,0:T(8,128)} %bitcast.29, bf16[768,256]{1,0:T(8,128)(2,1)} %constant.33.clone.refs_1_.refs_2_.refs_3_, bf16[96,288]{1,0:T(8,128)(2,1)} %constant.34.clone.refs_2_.refs_3_.refs_4_), custom_call_target="tpu_custom_call" | custom-call | flops 15000000512 | bytes 10000000 | tf_op jit(solution)/shard_map/comp0/pallas_call | solution.py:240
  105.2 1.1 copy-done.2
  106.3 7.2 %all-to-all-start.3 = ((f32[16,336,128]{2,1,0:T(8,128)}), f32[16,336,128]{2,1,0:T(8,128)S(1)}, u32[]{:S(2)}, u32[]{:S(2)}) async-start(f32[16,336,128]{2,1,0:T(8,128)} %bitcast.28), calls=%async_computation.3 | async-start | bytes 5505024 | tf_op jit(solution)/shard_map/all_to_all | solution.py:365
  113.4 25.4 %comp1.1 = f32[5376,128]{1,0:T(8,128)} custom-call(f32[2688,128]{1,0:T(8,128)} %bitcast.32, f32[96,3584]{1,0:T(8,128)} %get-tuple-element.31.refs_1_.refs_2_, bf16[768,256]{1,0:T(8,128)(2,1)} %constant.33.clone.refs_1_.refs_2_.refs_3_, bf16[96,288]{1,0:T(8,128)(2,1)} %constant.34.clone.refs_2_.refs_3_.refs_4_), custom_call_target="tpu_custom_call" | custom-call | flops 15000000512 | bytes 10000000 | tf_op jit(solution)/shard_map/comp1/pallas_call | solution.py:240
  138.8 10.3 %all-to-all-done.3 = f32[16,336,128]{2,1,0:T(8,128)S(1)} async-done(((f32[16,336,128]{2,1,0:T(8,128)}), f32[16,336,128]{2,1,0:T(8,128)S(1)}, u32[]{:S(2)}, u32[]{:S(2)}) %all-to-all-start.3) | async-done | bytes 2752544 | tf_op jit(solution)/shard_map/all_to_all | solution.py:365
  149.1 1.5 copy-done.1
  150.5 4.5 %all-to-all-start.4 = ((f32[16,336,128]{2,1,0:T(8,128)}), f32[16,336,128]{2,1,0:T(8,128)}, u32[]{:S(2)}, u32[]{:S(2)}) async-start(f32[16,336,128]{2,1,0:T(8,128)} %bitcast.27), calls=%async_computation.4 | async-start | bytes 5505024 | tf_op jit(solution)/shard_map/all_to_all | solution.py:365
  155.0 24.4 %comp2.1 = f32[2688,128]{1,0:T(8,128)} custom-call(s32[2]{0:T(128)} %pad_add_fusion.info.refs_0_, f32[2688,128]{1,0:T(8,128)} %bitcast.31, f32[96,3584]{1,0:T(8,128)} %get-tuple-element.31.refs_1_.refs_2_, bf16[768,256]{1,0:T(8,128)(2,1)} %constant.33.clone.refs_1_.refs_2_.refs_3_, bf16[96,288]{1,0:T(8,128)(2,1)} %constant.34.clone.refs_2_.refs_3_.refs_4_), custom_call_target="tpu_custom_call" | custom-call | flops 15000000512 | bytes 10000000 | tf_op jit(solution)/shard_map/comp2/pallas_call | solution.py:240
  179.4 14.0 %all-to-all-done.4 = f32[16,336,128]{2,1,0:T(8,128)} async-done(((f32[16,336,128]{2,1,0:T(8,128)}), f32[16,336,128]{2,1,0:T(8,128)}, u32[]{:S(2)}, u32[]{:S(2)}) %all-to-all-start.4) | async-done | bytes 2752544 | tf_op jit(solution)/shard_map/all_to_all | solution.py:365
  193.4 24.2 %all_to_all.52 = f32[16,168,128]{2,1,0:T(8,128)} all-to-all(f32[16,168,128]{2,1,0:T(8,128)} %bitcast.33), channel_id=1, replica_groups=mesh['dom'=16,'band'=8] {'dom'}, dimensions={0} | all-to-all | bytes 2752512 | tf_op jit(solution)/shard_map/all_to_all | solution.py:365
  217.5 8.0 %unpack.1 = (f32[6,40,3584]{2,1,0:T(8,128)}, f32[8,40,2688]{2,1,0:T(8,128)}, f32[8,40,2688]{2,1,0:T(8,128)}) custom-call(f32[5376,128]{1,0:T(8,128)} %bitcast.24, f32[5376,128]{1,0:T(8,128)} %bitcast.11.recv1, f32[2688,128]{1,0:T(8,128)} %bitcast.25), custom_call_target="tpu_custom_call" | custom-call | flops 4000000 | bytes 17000000 | tf_op jit(solution)/shard_map/unpack/pallas_call | solution.py:273
  225.5 46.2 %all_to_all.53 = f32[8,40,2688]{2,1,0:T(8,128)} all-to-all(f32[8,40,2688]{2,1,0:T(8,128)} %get-tuple-element.38), channel_id=1, replica_groups=mesh['dom'=16,'band'=8] {'band'}, dimensions={0} | all-to-all | bytes 6881280 | tf_op jit(solution)/shard_map/all_to_all | solution.py:388
  271.7 3.7 %all-to-all-start.7 = ((f32[8,40,2688]{2,1,0:T(8,128)}), f32[8,40,2688]{2,1,0:T(8,128)S(1)}, u32[]{:S(2)}, u32[]{:S(2)}) async-start(f32[8,40,2688]{2,1,0:T(8,128)} %get-tuple-element.41), calls=%async_computation.7 | async-start | bytes 6881280 | tf_op jit(solution)/shard_map/all_to_all | solution.py:390
  275.4 5.6 %overlap.1.inter = f32[320,320]{1,0:T(8,128)} custom-call(f32[320,2688]{1,0:T(8,128)} %bitcast.21), custom_call_target="tpu_custom_call" | custom-call | flops 2000000000 | bytes 4000000 | tf_op jit(solution)/shard_map/overlap/pallas_call | solution.py:313
  281.0 35.9 %all-to-all-done.7 = f32[8,40,2688]{2,1,0:T(8,128)S(1)} async-done(((f32[8,40,2688]{2,1,0:T(8,128)}), f32[8,40,2688]{2,1,0:T(8,128)S(1)}, u32[]{:S(2)}, u32[]{:S(2)}) %all-to-all-start.7) | async-done | bytes 3440672 | tf_op jit(solution)/shard_map/all_to_all | solution.py:390
  316.9 1.7 copy-done
  318.6 6.7 %energy.1 = f32[16,40,320]{2,1,0:T(8,128)} custom-call(f32[320,2688]{1,0:T(8,128)} %bitcast.22, f32[320,2688]{1,0:T(8,128)} %bitcast.23, f32[320,320]{1,0:T(8,128)} %overlap.1.inter), custom_call_target="tpu_custom_call" | custom-call | flops 2000000000 | bytes 8000000 | tf_op jit(solution)/shard_map/energy/pallas_call | solution.py:345
  325.3 20.0 %all_to_all.54 = f32[16,40,320]{2,1,0:T(8,128)S(1)} all-to-all(f32[16,40,320]{2,1,0:T(8,128)} %energy.1), channel_id=1, replica_groups=mesh['dom'=16,'band'=8] {'dom'}, dimensions={0} | all-to-all | bytes 1638400 | tf_op jit(solution)/shard_map/all_to_all | solution.py:394
  345.4 0.1 reduce_sum.18
  345.4 0.1 reshape.69
  345.6 0.2 reshape.72
  345.7 7.9 %all_to_all.55 = f32[8,1,1600]{2,1,0:T(1,128)S(1)} all-to-all(f32[8,1,1600]{2,1,0:T(1,128)S(1)} %reshape.72), channel_id=1, replica_groups=mesh['dom'=16,'band'=8] {'band'}, dimensions={0} | all-to-all | bytes 102400 | tf_op jit(solution)/shard_map/all_to_all | solution.py:396
  353.7 0.5 broadcast.1
  354.2 0.8 reduce
  355.0 0.1 reshape.73
  355.1 0.6 copy.10
  (9 shorter events, 0.1 us)
Async XLA Ops:
  8.5 43.6 %copy-start.3 = (f32[2688,128]{1,0:T(8,128)S(1)}, f32[2688,128]{1,0:T(8,128)}, u32[]{:S(2)}) copy-start(f32[2688,128]{1,0:T(8,128)} %get-tuple-element.24) | copy-start | bytes 4128772
  75.2 30.0 %all-to-all-start.2 = ((f32[16,168,128]{2,1,0:T(8,128)}), f32[16,168,128]{2,1,0:T(8,128)S(1)}, u32[]{:S(2)}, u32[]{:S(2)}) async-start(f32[16,168,128]{2,1,0:T(8,128)} %bitcast.6), calls=%async_computation.2 | async-start | bytes 2752512 | tf_op jit(solution)/shard_map/all_to_all | solution.py:365
  105.2 1.1 copy-start.2
  106.3 42.8 %all-to-all-start.3 = ((f32[16,336,128]{2,1,0:T(8,128)}), f32[16,336,128]{2,1,0:T(8,128)S(1)}, u32[]{:S(2)}, u32[]{:S(2)}) async-start(f32[16,336,128]{2,1,0:T(8,128)} %bitcast.28), calls=%async_computation.3 | async-start | bytes 5505024 | tf_op jit(solution)/shard_map/all_to_all | solution.py:365
  149.1 1.5 copy-start.1
  150.5 42.8 %all-to-all-start.4 = ((f32[16,336,128]{2,1,0:T(8,128)}), f32[16,336,128]{2,1,0:T(8,128)}, u32[]{:S(2)}, u32[]{:S(2)}) async-start(f32[16,336,128]{2,1,0:T(8,128)} %bitcast.27), calls=%async_computation.4 | async-start | bytes 5505024 | tf_op jit(solution)/shard_map/all_to_all | solution.py:365
  271.7 45.2 %all-to-all-start.7 = ((f32[8,40,2688]{2,1,0:T(8,128)}), f32[8,40,2688]{2,1,0:T(8,128)S(1)}, u32[]{:S(2)}, u32[]{:S(2)}) async-start(f32[8,40,2688]{2,1,0:T(8,128)} %get-tuple-element.41), calls=%async_computation.7 | async-start | bytes 6881280 | tf_op jit(solution)/shard_map/all_to_all | solution.py:390
  316.9 1.7 copy-start

commit v2 on v1

v2 whole, which is shorter than its diff:
```python
import math

import jax
import jax.numpy as jnp
import ml_dtypes
import numpy as np
from jax import lax
from jax.experimental import pallas as pl
from jax.experimental.pallas import tpu as pltpu
from jax.sharding import PartitionSpec as P

NY = 56
NZ = 64
NX = 96
CELLS = NY * NZ
TILES = CELLS // 128
CAP = 40
PLANES = 6
EDGE = 384
WIDE = CELLS + 2 * EDGE
ROWS = PLANES * TILES
HALF = 16
QUAD = 4
GROUP = 512
LINE = TILES + QUAD
PARTS = 21
MAIN = 32
SHARE = 11
VMEM = 60 * 1024 * 1024
F32 = jnp.float32
BF16 = jnp.bfloat16


def stencil_weights():
    fact = math.factorial
    sides = [
        2.0 * (-1.0) ** (k + 1) * fact(6) ** 2 / (k * k * fact(6 - k) * fact(6 + k))
        for k in range(1, 7)
    ]
    return (-2.0 * sum(sides), sides)


CENTER, SIDES = stencil_weights()
KINETIC = -0.5 * (1.0 / 0.36)
SCALE = 2.0 / 11.0
STEP = [SCALE * KINETIC * s for s in SIDES]


def halves(matrix):
    exact = matrix.astype(np.float32)
    high = exact.astype(ml_dtypes.bfloat16)
    low = (exact - high.astype(np.float32)).astype(ml_dtypes.bfloat16)
    return high, low


def band_matrix(size):
    out = np.zeros((size, size))
    for k in range(1, 7):
        for i in range(size - k):
            out[i, i + k] = out[i + k, i] = STEP[k - 1]
    return out


def stencil_operands():
    zh, zl = halves(np.kron(np.eye(4), band_matrix(NZ)))
    xh, xl = halves(band_matrix(NX))
    return np.concatenate([zh, zh, zl], axis=0), np.concatenate([xh, xh, xl], axis=1)


def cost(flops, nbytes):
    return pl.CostEstimate(flops=flops, transcendentals=0, bytes_accessed=nbytes)


def params():
    return pltpu.CompilerParams(vmem_limit_bytes=VMEM)


SMEM_SPEC = pl.BlockSpec(memory_space=pltpu.SMEM)


def pack_body(info, states, pot, out0, out1, out2):
    live = info[0]
    lanes = lax.broadcasted_iota(jnp.int32, (8, 128), 0)
    first = pl.multiple_of(jnp.minimum(info[2], 6) * (QUAD * 128), 128)
    for p in range(PLANES):
        tiles = [pot[p : p + 1, pl.ds(first + e * 128, 128)] for e in range(QUAD)]
        piece = jnp.concatenate(tiles, axis=0)
        for d in range(16):
            base = (d * PLANES + p) * LINE + TILES
            out0[base : base + QUAD, :] = piece

    def plane(p, carry):
        for i in range(5):
            keep = (lanes + 8 * i) < live
            for r in range(TILES):
                v = states[p, 8 * i : 8 * i + 8, r * 128 : (r + 1) * 128]
                v = jnp.where(keep, v, 0.0)
                if i < 2:
                    out0[pl.ds(8 * i * PLANES * LINE + p * LINE + r, 8, stride=PLANES * LINE), :] = v
                elif i < 4:
                    out1[pl.ds(8 * (i - 2) * ROWS + p * TILES + r, 8, stride=ROWS), :] = v
                else:
                    for q in range(2):
                        out2[pl.ds(8 * q * ROWS + p * TILES + r, 8, stride=ROWS), :] = v
        return carry

    lax.fori_loop(0, PLANES, plane, 0)


def pack(info, states, pot):
    return pl.pallas_call(
        pack_body,
        out_shape=(
            jax.ShapeDtypeStruct((NX * LINE, 128), F32),
            jax.ShapeDtypeStruct((16 * ROWS, 128), F32),
            jax.ShapeDtypeStruct((16 * ROWS, 128), F32),
        ),
        in_specs=[SMEM_SPEC, pl.BlockSpec(), pl.BlockSpec()],
        compiler_params=params(),
        cost_estimate=cost(4_000_000, 10_000_000),
        name="pack",
    )(info, states, pot)


def split(value):
    high = value.astype(BF16)
    return high, (value - high.astype(F32)).astype(BF16)


def comp_body(first, half, *refs):
    if first:
        info, recv = refs[:2]
        pots = refs[2:10]
        wz, ax, out, image, diag = refs[10:15]
        refs = refs[15:]
    elif half:
        info, recv, diag, wz, ax, out, image, part = refs[:8]
        refs = refs[8:]
    else:
        recv, diag, wz, ax, out, image = refs[:6]
        refs = refs[6:]
    va, vb, ua, ub, ha, hb, la, lb, az, ay = refs
    stride = LINE if first else TILES
    zero = jnp.zeros((NX, EDGE), F32)
    for ref in (va, vb, ua, ub):
        ref[:, :EDGE] = zero
        ref[:, EDGE + CELLS :] = zero

    def load(r, carry):
        at = pl.multiple_of(r * 128, 128)
        tiles = [recv[pl.ds(8 * i * stride + r, 8, stride=stride), :] for i in range(12)]
        v = jnp.concatenate(tiles, axis=0)
        va[:, pl.ds(EDGE + at, 128)] = v
        ua[:, pl.ds(EDGE + at, 128)] = pltpu.roll(v, 64, 1)
        high, low = split(v)
        ha[:, pl.ds(at, 128)] = high
        la[:, pl.ds(at, 128)] = low
        return carry

    lax.fori_loop(0, TILES, load, 0)
    if first:
        for s in range(8):
            whose = info[2] ^ s

            @pl.when(whose < 7)
            def _():
                for e in range(QUAD):
                    at = pl.multiple_of(whose * (QUAD * 128) + e * 128, 128)
                    tiles = [
                        pots[s][pl.ds(8 * i * QUAD + e, 8, stride=QUAD), :] for i in range(12)
                    ]
                    diag[:, pl.ds(at, 128)] = (
                        SCALE * (jnp.concatenate(tiles, axis=0) + KINETIC * 3.0 * CENTER) - 2.0
                    )

    low_half = (lax.broadcasted_iota(jnp.int32, (8, GROUP), 1) % 128) < 64

    def apply(src, dst, stage):
        v_src, u_src, h_src, l_src = src
        v_dst, u_dst, h_dst, l_dst = dst

        def products(at):
            lefts = []
            for j in range(GROUP // 256):
                h = h_src[:, pl.ds(at + 256 * j, 256)]
                l = l_src[:, pl.ds(at + 256 * j, 256)]
                lefts.append(jnp.concatenate([h, l, h], axis=1))
            along_z = jnp.dot(
                jnp.concatenate(lefts, axis=0), wz[...], preferred_element_type=F32
            )
            h = h_src[:, pl.ds(at, GROUP)]
            l = l_src[:, pl.ds(at, GROUP)]
            along_x = jnp.dot(
                ax[...], jnp.concatenate([h, l, h], axis=0), preferred_element_type=F32
            )
            return along_z, along_x

        az[...], ay[...] = products(0)

        def block(group, carry):
            at = pl.multiple_of(group * GROUP, GROUP)
            after = jnp.minimum(group + 1, CELLS // GROUP - 1)
            next_z, next_x = products(pl.multiple_of(after * GROUP, GROUP))
            pending = []
            for i in range(12):
                rows = slice(8 * i, 8 * i + 8)
                v = v_src[rows, pl.ds(at, GROUP + 2 * EDGE)]
                u = u_src[rows, pl.ds(at, GROUP + 2 * EDGE)]

                def v_at(k):
                    return v[:, EDGE + 128 * k : EDGE + 128 * k + GROUP]

                def u_at(k):
                    return u[:, EDGE + 128 * k : EDGE + 128 * k + GROUP + 128]

                odd = STEP[0] * (u_at(0) + u_at(-1))
                odd = odd + STEP[2] * (u_at(1) + u_at(-2))
                odd = odd + STEP[4] * (u_at(2) + u_at(-3))
                even = STEP[1] * (v_at(1) + v_at(-1))
                even = even + STEP[3] * (v_at(2) + v_at(-2))
                even = even + STEP[5] * (v_at(3) + v_at(-3))
                near = even + jnp.where(low_half, odd[:, :GROUP], odd[:, 128:])
                center = v_at(0)
                new = near + diag[rows, pl.ds(at, GROUP)] * center
                new = new + ay[rows, :]
                across = [slice(NX * j + 8 * i, NX * j + 8 * i + 8) for j in range(GROUP // 256)]
                new = new + jnp.concatenate([az[strip, :] for strip in across], axis=1)
                ay[rows, :] = next_x[rows, :]
                for strip in across:
                    az[strip, :] = next_z[strip, :]
                if stage == 1:
                    new = 0.5 * new
                elif stage < 4:
                    new = new - v_dst[rows, pl.ds(EDGE + at, GROUP)]
                else:
                    new = 5.5 * new + 11.0 * center
                v_dst[rows, pl.ds(EDGE + at, GROUP)] = new
                if stage < 4:
                    for j in range(GROUP // 128):
                        u_dst[rows, pl.ds(EDGE + at + 128 * j, 128)] = pltpu.roll(
                            new[:, 128 * j : 128 * j + 128], 64, 1
                        )
                    pending.append(new)
                    if i % 2:
                        high, low = split(jnp.concatenate(pending, axis=0))
                        pair = slice(8 * i - 8, 8 * i + 8)
                        h_dst[pair, pl.ds(at, GROUP)] = high
                        l_dst[pair, pl.ds(at, GROUP)] = low
                        pending = []
            return carry

        lax.fori_loop(0, CELLS // GROUP, block, 0)

    a, b = (va, ua, ha, la), (vb, ub, hb, lb)
    apply(a, b, 1)
    apply(b, a, 2)
    apply(a, b, 3)
    apply(b, a, 4)
    outs = [(out, 1, 0), (image, 0, 0)]
    if half:
        outs.append((part, 1, info[1] * (12 * 128)))

    for ref, which, begin in outs:
        count = ref.shape[0] // NX

        def store(r, carry):
            at = pl.multiple_of(EDGE + begin + r * 128, 128)
            for i in range(12):
                ref[pl.ds(8 * i * count + r, 8, stride=count), :] = (vb if which else va)[
                    8 * i : 8 * i + 8, pl.ds(at, 128)
                ]
            return carry

        lax.fori_loop(0, count, store, 0)


def comp(first, half, args):
    out_shape = [jax.ShapeDtypeStruct((NX * TILES, 128), F32)] * 2
    if first:
        out_shape.append(jax.ShapeDtypeStruct((NX, CELLS), F32))
    if half:
        out_shape.append(jax.ShapeDtypeStruct((NX * HALF, 128), F32))
    wide = pltpu.VMEM((NX, WIDE), F32)
    narrow = pltpu.VMEM((NX, CELLS), BF16)
    in_specs = [pl.BlockSpec()] * len(args)
    if first or half:
        in_specs[0] = SMEM_SPEC

    def body(*refs):
        comp_body(first, half, *refs)

    return pl.pallas_call(
        body,
        out_shape=tuple(out_shape),
        in_specs=in_specs,
        scratch_shapes=[wide] * 4
        + [narrow] * 4
        + [pltpu.VMEM((NX * GROUP // 256, 256), F32), pltpu.VMEM((NX, GROUP), F32)],
        compiler_params=params(),
        cost_estimate=cost(15_000_000_000, 10_000_000),
    )(*args)


def unpack_main_body(later, *refs):
    info, recv = refs[:2]
    filtered, *sends = refs[3:12] if later else refs[2:11]
    send = refs[-1]
    for p in range(PLANES):
        for r in range(TILES):
            b, t = divmod(p * TILES + r, PARTS)
            for i in range(2):
                v = recv[pl.ds(8 * i * ROWS + p * TILES + r, 8, stride=ROWS), :]
                rows = slice(8 * i, 8 * i + 8)
                send[b ^ info[2], rows, t * 128 : (t + 1) * 128] = v
                filtered[p, rows, r * 128 : (r + 1) * 128] = v
    for s in range(8):
        sends[s][...] = send[s]


def unpack_main(info, recv, base):
    later = base is not None
    which = int(later)

    def body(*refs):
        unpack_main_body(later, *refs)

    in_specs = [SMEM_SPEC, pl.BlockSpec((16 * ROWS, 128), lambda i: (0, 0))]
    args = (info, recv)
    if later:
        in_specs.append(pl.BlockSpec(memory_space=pl.ANY))
        args += (base,)
    return pl.pallas_call(
        body,
        grid=(1,),
        out_shape=(jax.ShapeDtypeStruct((PLANES, CAP, CELLS), F32),)
        + (jax.ShapeDtypeStruct((16, PARTS * 128), F32),) * 8,
        in_specs=in_specs,
        out_specs=(pl.BlockSpec((PLANES, 16, CELLS), lambda i: (0, which, 0)),)
        + (pl.BlockSpec((16, PARTS * 128), lambda i: (0, 0)),) * 8,
        scratch_shapes=[pltpu.VMEM((8, 16, PARTS * 128), F32)],
        input_output_aliases={2: 0} if later else {},
        compiler_params=params(),
        cost_estimate=cost(4_000_000, 4_000_000),
    )(*args)


def unpack_rest_body(recv, base, filtered):
    for p in range(PLANES):
        for r in range(TILES):
            q = r // HALF
            start = 8 * q * PLANES * HALF + p * HALF + r - 12 * q
            filtered[p, :, r * 128 : (r + 1) * 128] = recv[
                pl.ds(start, 8, stride=PLANES * HALF), :
            ]


def unpack_rest(recv, base):
    return pl.pallas_call(
        unpack_rest_body,
        grid=(1,),
        out_shape=jax.ShapeDtypeStruct((PLANES, CAP, CELLS), F32),
        in_specs=[
            pl.BlockSpec((16 * PLANES * HALF, 128), lambda i: (0, 0)),
            pl.BlockSpec(memory_space=pl.ANY),
        ],
        out_specs=pl.BlockSpec((PLANES, 8, CELLS), lambda i: (0, 4, 0)),
        input_output_aliases={1: 0},
        compiler_params=params(),
        cost_estimate=cost(1_000_000, 2_000_000),
        name="unpack_rest",
    )(recv, base)


def share_body(info, img0, img1, img2, f2, out):
    second = info[1] > 0

    def group(big, carry):
        base = pl.multiple_of(big * 8 * PARTS, 8)
        to = pl.multiple_of(big * 8 * 64, 8)
        for g in range(8):
            at = base + PARTS * g
            row = to + 64 * g
            out[pl.ds(row, PARTS), :] = img0[pl.ds(at, PARTS), :]
            out[pl.ds(row + PARTS, PARTS), :] = img1[pl.ds(at, PARTS), :]
            for ref, start in ((img2, 2 * PARTS), (f2, 2 * PARTS + SHARE)):
                out[pl.ds(row + start, SHARE), :] = jnp.where(
                    second, ref[pl.ds(at + 10, SHARE), :], ref[pl.ds(at, SHARE), :]
                )
        return carry

    lax.fori_loop(0, 16, group, 0)


def share(info, img0, img1, img2, f2):
    return pl.pallas_call(
        share_body,
        out_shape=jax.ShapeDtypeStruct((128 * 64, 128), F32),
        in_specs=[SMEM_SPEC] + [pl.BlockSpec()] * 4,
        compiler_params=params(),
        cost_estimate=cost(2_000_000, 10_000_000),
        name="share",
    )(info, img0, img1, img2, f2)


SLOTS = 8 * CAP
SECOND = 384
BOTH = SECOND + SLOTS
KSTEP = 7 * 128


def gram_body(info, *refs):
    pieces, (rest, out, main, high, low, total) = refs[:16], refs[16:]
    for s in range(8):
        for k in range(2):
            main[info[2] ^ s, 16 * k : 16 * k + 16] = pieces[8 * k + s][...]
    high[SLOTS:SECOND, :] = jnp.zeros((SECOND - SLOTS, PARTS * 128), BF16)
    low[SLOTS:SECOND, :] = jnp.zeros((SECOND - SLOTS, PARTS * 128), BF16)

    def fill(t, carry, late):
        at = pl.multiple_of(t * 128, 128)
        f_rows = []
        i_rows = []
        for b in range(8):
            shared = [
                rest[
                    pl.ds((8 * late * 8 + b) * 64 + start + t - 10 * late, 8, stride=8 * 64), :
                ]
                for start in (2 * PARTS, 2 * PARTS + SHARE)
            ]
            f_rows += [main[b, :, pl.ds(at, 128)], shared[1]]
            for k in range(2):
                for half in range(2):
                    start = (64 * half + b) * 64 + PARTS * k + t
                    i_rows.append(rest[pl.ds(start, 8, stride=8 * 64), :])
            i_rows.append(shared[0])
        for rows, base in ((f_rows, 0), (i_rows, SECOND)):
            h, l = split(jnp.concatenate(rows, axis=0))
            high[base : base + SLOTS, pl.ds(at, 128)] = h
            low[base : base + SLOTS, pl.ds(at, 128)] = l
        return carry

    lax.fori_loop(0, SHARE, lambda t, c: fill(t, c, 0), 0)
    lax.fori_loop(SHARE, PARTS, lambda t, c: fill(t, c, 1), 0)
    for step in range(3):
        cols = slice(step * KSTEP, (step + 1) * KSTEP)
        term = None
        for one, two in ((high, high), (high, low), (low, high)):
            part = lax.dot_general(
                one[:SLOTS, cols],
                two[:, cols],
                (((1,), (1,)), ((), ())),
                preferred_element_type=F32,
            )
            term = part if term is None else term + part
        total[...] = term if step == 0 else total[...] + term
    for d in range(16):
        out[d, :20, :] = total[20 * d : 20 * d + 20, :SLOTS]
        out[d, 20:40, :] = total[20 * d : 20 * d + 20, SECOND:]


def gram(info, pieces, rest):
    return pl.pallas_call(
        gram_body,
        out_shape=jax.ShapeDtypeStruct((16, 40, SLOTS), F32),
        in_specs=[SMEM_SPEC] + [pl.BlockSpec()] * 17,
        scratch_shapes=[pltpu.VMEM((8, MAIN, PARTS * 128), F32)]
        + [pltpu.VMEM((BOTH, PARTS * 128), BF16)] * 2
        + [pltpu.VMEM((SLOTS, BOTH), F32)],
        compiler_params=params(),
        cost_estimate=cost(4_000_000_000, 8_000_000),
        name="gram",
    )(info, *pieces, rest)


def exchange(value, axis, parts):
    shape = value.shape
    value = value.reshape((parts, -1) + shape[-1:])
    return lax.all_to_all(value, axis, 0, 0, tiled=True).reshape(shape)


def swaps(pieces):
    out = [pieces[0]]
    for s in range(1, 8):
        pairs = [(b, b ^ s) for b in range(8)]
        out.append(lax.ppermute(pieces[s], "band", pairs))
    return out


def work(states, potential, counts):
    wz, ax = (jnp.asarray(m) for m in stencil_operands())
    band = lax.axis_index("band")
    info = jnp.stack([counts[band], lax.axis_index("dom") // 8, band]).astype(jnp.int32)
    send0, send1, send2 = pack(info, jnp.transpose(states, (1, 0, 2)), potential)
    recv0 = exchange(send0, "dom", 16)
    own = recv0.reshape(NX, LINE, 128)[:, TILES:, :].reshape(NX * QUAD, 128)
    pots = swaps([own] * 8)
    recv0, send1 = lax.optimization_barrier((recv0, send1))
    recv1 = exchange(send1, "dom", 16)
    out0, img0, diag = comp(True, False, (info, recv0, *pots, wz, ax))
    recv1, send2 = lax.optimization_barrier((recv1, send2))
    recv2 = exchange(send2, "dom", 16)
    out1, img1 = comp(False, False, (recv1, diag, wz, ax))
    recv2, out0 = lax.optimization_barrier((recv2, out0))
    back0 = exchange(out0, "dom", 16)
    filtered, *early = unpack_main(info, back0, None)
    early = swaps(early)
    recv2, filtered = lax.optimization_barrier((recv2, filtered))
    out2, img2, half2 = comp(False, True, (info, recv2, diag, wz, ax))
    back0, out1 = lax.optimization_barrier((back0, out1))
    back1 = exchange(out1, "dom", 16)
    back1, half2 = lax.optimization_barrier((back1, half2))
    back2 = exchange(half2, "dom", 16)
    filtered, *late = unpack_main(info, back1, filtered)
    late = swaps(late)
    img0, filtered = lax.optimization_barrier((img0, filtered))
    shared = share(info, img0, img1, img2, out2)
    back2, shared = lax.optimization_barrier((back2, shared))
    filtered = unpack_rest(back2, filtered)
    rest = exchange(shared, ("dom", "band"), 128)
    terms = gram(info, early + late, rest)
    terms = lax.all_to_all(terms, "dom", 0, 0, tiled=True).sum(axis=0)
    terms = jnp.transpose(terms.reshape(2, 20, 8, CAP), (2, 0, 1, 3)).reshape(8, 40, CAP)
    terms = lax.all_to_all(terms, "band", 0, 0, tiled=True).sum(axis=0)
    projected = jnp.transpose(terms.reshape(2, 20, CAP), (0, 2, 1))
    return (jnp.transpose(filtered, (1, 0, 2)), projected)


def solution(mesh):
    return jax.shard_map(
        work,
        mesh=mesh,
        in_specs=(P("band", "dom", None), P("dom", None), P()),
        out_specs=(P("band", "dom", None), P(None, "band", "dom")),
        check_vma=False,
    )
```

time: 357 us -> 310 us (0.87)
  blocking collectives: 165 us -> 54.7 us
  starting transfers between devices: 19 us -> 58.8 us
  waiting for transfers between devices: 60.1 us -> 95.8 us
  Pallas kernels: 102 us -> 87.1 us
    ppermute x0 -> x21, waiting for transfers between devices: none -> 68.3 us  [swaps(): out.append(lax.ppermute(pieces[s], 'band', pairs))]
    all_to_all x3 -> x1, blocking collectives: 90.9 us -> 30.8 us  [exchange(): return lax.all_to_all(value, axis, 0, 0, tiled=True).reshape(shape)]
    all_to_all x3 -> x1, blocking collectives: 74.1 us -> 23.9 us  [work(): terms = lax.all_to_all(terms, 'dom', 0, 0, tiled=True).sum(axis=0)]
    all_to_all x1, waiting for transfers between devices: 35.9 us -> 3.09 us  [work(): terms = lax.all_to_all(terms, 'band', 0, 0, tiled=True).sum(axis=0)]
    ppermute x0 -> x21, starting transfers between devices: none -> 26.3 us  [swaps(): out.append(lax.ppermute(pieces[s], 'band', pairs))]
    pallas_call x3, Pallas kernels: 76 us -> 55.4 us  [comp(): pl.pallas_call(body, out_shape=tuple(out_shape), in_specs=in_specs, scrat...]
    all_to_all x3 -> x6, starting transfers between devices: 15.3 us -> 29.2 us  [exchange(): return lax.all_to_all(value, axis, 0, 0, tiled=True).reshape(shape)]
    pallas_call x4 -> x6, Pallas kernels: 25.8 us -> 31.7 us  [the longest x1 12.5 us: gram(): pl.pallas_call(gram_body, out_shape=jax.ShapeDtypeStruct((16, 40, SLOTS),...]
  transfers between devices with their start and end apart: 4 -> 28, of which waited for: 3 -> 15; matrix products, arithmetic and copies ran while one was open for 0% -> 0% of each run, Pallas kernels for 23% -> 21%
where the time goes in v2:
time: 310 us; the launch traced here: 308 us
  waiting for transfers between devices  95.8 us (31%)
  Pallas kernels  87.1 us (28%)
  starting transfers between devices  58.8 us (19%)
  blocking collectives  54.7 us (18%)
  local copies, waits for them, and re-layouts  8.36 us (3%)
    ppermute x21, waiting for transfers between devices, swaps(): out.append(lax.ppermute(pieces[s], 'band', pairs))  68.3 us
    pallas_call x3, Pallas kernels, comp(): pl.pallas_call(body, out_shape=tuple(out_shape), in_specs=in_specs, scrat...  55.4 us
    all_to_all x1, blocking collectives, exchange(): return lax.all_to_all(value, axis, 0, 0, tiled=True).reshape(shape)  30.8 us
    all_to_all x6, starting transfers between devices, exchange(): return lax.all_to_all(value, axis, 0, 0, tiled=True).reshape(shape)  29.2 us
    ppermute x21, starting transfers between devices, swaps(): out.append(lax.ppermute(pieces[s], 'band', pairs))  26.3 us
    all_to_all x6, waiting for transfers between devices, exchange(): return lax.all_to_all(value, axis, 0, 0, tiled=True).reshape(shape)  24.3 us
    all_to_all x1, blocking collectives, work(): terms = lax.all_to_all(terms, 'dom', 0, 0, tiled=True).sum(axis=0)  23.9 us
    pallas_call x1, Pallas kernels, gram(): pl.pallas_call(gram_body, out_shape=jax.ShapeDtypeStruct((16, 40, SLOTS),...  12.5 us
  transfers between devices with their start and end apart: 28, of which 15 were waited for; matrix products, arithmetic and copies ran while one was open for 0% of the time, Pallas kernels for 21%

profile of v2, /device:TPU:0, one launch (start us, length us, event | category | flops | bytes accessed | tf_op | source)
XLA Modules:
  0.0 307.9 jit_solution(15066173271812430788)
XLA Ops:
  3.2 5.3 %pack.1 = (f32[3072,128]{1,0:T(8,128)}, f32[2688,128]{1,0:T(8,128)}, f32[2688,128]{1,0:T(8,128)}) custom-call(s32[3]{0:T(128)} %pad_add_fusion.info.refs_0_, f32[6,40,3584]{2,1,0:T(8,128)} %bitcast.28, f32[6,3584]{1,0:T(8,128)} %pot.1), custom_call_target="tpu_custom_call" | custom-call | flops 4000000 | bytes 10000000 | tf_op jit(solution)/shard_map/pack/pallas_call | solution.py:111
  8.5 30.8 %all_to_all.45 = f32[16,192,128]{2,1,0:T(8,128)S(1)} all-to-all(f32[16,192,128]{2,1,0:T(8,128)} %bitcast.32), channel_id=1, replica_groups=mesh['dom'=16,'band'=8] {'dom'}, dimensions={0} | all-to-all | bytes 3145728 | tf_op jit(solution)/shard_map/all_to_all | solution.py:478
  39.3 3.7 %all-to-all-start.1 = ((f32[16,168,128]{2,1,0:T(8,128)}), f32[16,168,128]{2,1,0:T(8,128)S(1)}, u32[]{:S(2)}, u32[]{:S(2)}) async-start(f32[16,168,128]{2,1,0:T(8,128)} %bitcast.36), calls=%async_computation.1 | async-start | bytes 2752512 | tf_op jit(solution)/shard_map/all_to_all | solution.py:478
  45.0 3.2 %collective-permute-start.3 = (f32[384,128]{1,0:T(8,128)S(1)}, f32[384,128]{1,0:T(8,128)}, u32[]{:S(2)}, u32[]{:S(2)}) collective-permute-start(f32[384,128]{1,0:T(8,128)S(1)} %bitcast.43), channel_id=1, source_target_pairs={{0,4},{1,5},{2,6},{3,7},{4,0},{5,1},{6,2},{7,3},{8,12},{9,13},{10,... | collective-permute-start | bytes 589832 | tf_op jit(solution)/shard_map/ppermute | solution.py:485
  48.3 3.0 collective-permute-start.5
  52.7 10.4 %all-to-all-done.1 = f32[16,168,128]{2,1,0:T(8,128)S(1)} async-done(((f32[16,168,128]{2,1,0:T(8,128)}), f32[16,168,128]{2,1,0:T(8,128)S(1)}, u32[]{:S(2)}, u32[]{:S(2)}) %all-to-all-start.1) | async-done | bytes 1376288 | tf_op jit(solution)/shard_map/all_to_all | solution.py:478
  64.3 3.7 %all-to-all-start.2 = ((f32[16,168,128]{2,1,0:T(8,128)}), f32[16,168,128]{2,1,0:T(8,128)S(1)}, u32[]{:S(2)}, u32[]{:S(2)}) async-start(f32[16,168,128]{2,1,0:T(8,128)} %bitcast.34), calls=%async_computation.2 | async-start | bytes 2752512 | tf_op jit(solution)/shard_map/all_to_all | solution.py:478
  69.0 19.9 %shard_map.68 = (f32[2688,128]{1,0:T(8,128)}, f32[2688,128]{1,0:T(8,128)}, f32[96,3584]{1,0:T(8,128)}) custom-call(s32[3]{0:T(128)} %pad_add_fusion.info.refs_0_, f32[3072,128]{1,0:T(8,128)} %bitcast.31, f32[384,128]{1,0:T(8,128)} %bitcast.47, f32[384,128]{1,0:T(8,128)} %copy-done.7, f32[384,128]{1,0:T(8,128)} %copy-done.8, f32[384,128]{1,0:T(8,128)} %copy-done.9, ...), custom_call_target="tpu_custom_call" | custom-call | flops 15000000512 | bytes 10000000 | tf_op jit(solution)/shard_map/pallas_call | solution.py:292
  90.0 7.1 %all-to-all-start.3 = ((f32[16,168,128]{2,1,0:T(8,128)}), f32[16,168,128]{2,1,0:T(8,128)S(1)}, u32[]{:S(2)}, u32[]{:S(2)}) async-start(f32[16,168,128]{2,1,0:T(8,128)} %bitcast.37), calls=%async_computation.3 | async-start | bytes 2752512 | tf_op jit(solution)/shard_map/all_to_all | solution.py:478
  97.1 17.4 %shard_map.69 = (f32[2688,128]{1,0:T(8,128)}, f32[2688,128]{1,0:T(8,128)}) custom-call(f32[2688,128]{1,0:T(8,128)} %bitcast.33, f32[96,3584]{1,0:T(8,128)} %get-tuple-element.55.refs_1_.refs_2_, bf16[768,256]{1,0:T(8,128)(2,1)} %constant.33.clone.refs_10_.refs_2_.refs_3_, bf16[96,288]{1,0:T(8,128)(2,1)} %constant.34.clone.refs_11_.refs_3_.refs_4_), custom_call_target="tpu_custom_call" | custom-call | flops 15000000512 | bytes 10000000 | tf_op jit(solution)/shard_map/pallas_call | solution.py:292
  114.5 5.5 %all-to-all-done.3 = f32[16,168,128]{2,1,0:T(8,128)S(1)} async-done(((f32[16,168,128]{2,1,0:T(8,128)}), f32[16,168,128]{2,1,0:T(8,128)S(1)}, u32[]{:S(2)}, u32[]{:S(2)}) %all-to-all-start.3) | async-done | bytes 1376288 | tf_op jit(solution)/shard_map/all_to_all | solution.py:478
  121.2 3.2 %shard_map.70 = (f32[6,40,3584]{2,1,0:T(8,128)}, f32[16,2688]{1,0:T(8,128)}, f32[16,2688]{1,0:T(8,128)}, f32[16,2688]{1,0:T(8,128)}, f32[16,2688]{1,0:T(8,128)},...) custom-call(s32[3]{0:T(128)} %pad_add_fusion.info.refs_0_, ...), custom_call_target="tpu_custom_call" | custom-call | flops 4000000 | bytes 4000000 | tf_op jit(solution)/shard_map/pallas_call | solution.py:332
  124.4 3.7 %all-to-all-start.4 = ((f32[16,168,128]{2,1,0:T(8,128)}), f32[16,168,128]{2,1,0:T(8,128)S(1)}, u32[]{:S(2)}, u32[]{:S(2)}) async-start(f32[16,168,128]{2,1,0:T(8,128)} %bitcast.13), calls=%async_computation.4 | async-start | bytes 2752512 | tf_op jit(solution)/shard_map/all_to_all | solution.py:478
  128.1 18.1 %shard_map.71 = (f32[2688,128]{1,0:T(8,128)}, f32[2688,128]{1,0:T(8,128)}, f32[1536,128]{1,0:T(8,128)}) custom-call(s32[3]{0:T(128)} %pad_add_fusion.info.refs_0_, f32[2688,128]{1,0:T(8,128)} %bitcast.35, f32[96,3584]{1,0:T(8,128)} %get-tuple-element.55.refs_1_.refs_2_, bf16[768,256]{1,0:T(8,128)(2,1)} %constant.33.clone.refs_10_.refs_2_.refs_3_, ...), custom_call_target="tpu_custom_call" | custom-call | flops 15000000512 | bytes 10000000 | tf_op jit(solution)/shard_map/pallas_call | solution.py:292
  146.3 3.1 all-to-all-done.4
  149.3 4.1 %all-to-all-start.5 = ((f32[16,96,128]{2,1,0:T(8,128)}), f32[16,96,128]{2,1,0:T(8,128)S(1)}, u32[]{:S(2)}, u32[]{:S(2)}) async-start(f32[16,96,128]{2,1,0:T(8,128)} %bitcast.38), calls=%async_computation.5 | async-start | bytes 1572864 | tf_op jit(solution)/shard_map/all_to_all | solution.py:478
  153.4 3.2 %shard_map.72 = (f32[6,40,3584]{2,1,0:T(8,128)}, f32[16,2688]{1,0:T(8,128)}, f32[16,2688]{1,0:T(8,128)}, f32[16,2688]{1,0:T(8,128)}, f32[16,2688]{1,0:T(8,128)},...) custom-call(s32[3]{0:T(128)} %pad_add_fusion.info.refs_0_, ...), custom_call_target="tpu_custom_call", output_to_operand_aliasing={{0}: (2, {})} | custom-call | flops 4000000 | bytes 4000000 | tf_op jit(solution)/shard_map/pallas_call | solution.py:332
  156.7 5.1 %share.1 = f32[8192,128]{1,0:T(8,128)} custom-call(s32[3]{0:T(128)} %pad_add_fusion.info.refs_0_, f32[2688,128]{1,0:T(8,128)} %get-tuple-element.67.img0, f32[2688,128]{1,0:T(8,128)} %get-tuple-element.68.img1, f32[2688,128]{1,0:T(8,128)} %get-tuple-element.69.img2, f32[2688,128]{1,0:T(8,128)} %get-tuple-element.70.f2), custom_call_target="tpu_custom_call" | custom-call | flops 2000000 | bytes 10000000 | tf_op jit(solution)/shard_map/share/pallas_call | solution.py:395
  161.7 5.3 %all-to-all-done.5 = f32[16,96,128]{2,1,0:T(8,128)S(1)} async-done(((f32[16,96,128]{2,1,0:T(8,128)}), f32[16,96,128]{2,1,0:T(8,128)S(1)}, u32[]{:S(2)}, u32[]{:S(2)}) %all-to-all-start.5) | async-done | bytes 786464 | tf_op jit(solution)/shard_map/all_to_all | solution.py:478
  167.9 6.8 %all-to-all-start.6 = ((f32[128,64,128]{2,1,0:T(8,128)}), f32[128,64,128]{2,1,0:T(8,128)}, u32[]{:S(2)}, u32[]{:S(2)}) async-start(f32[128,64,128]{2,1,0:T(8,128)} %bitcast.24), calls=%async_computation.6 | async-start | bytes 8388608 | tf_op jit(solution)/shard_map/all_to_all | solution.py:478
  176.7 2.4 collective-permute-start.10
  182.2 42.5 %collective-permute-done.8.refs_2_ = f32[16,2688]{1,0:T(8,128)S(1)} collective-permute-done((f32[16,2688]{1,0:T(8,128)S(1)}, f32[16,2688]{1,0:T(8,128)S(1)}, u32[]{:S(2)}, u32[]{:S(2)}) %collective-permute-start.8) | collective-permute-done | bytes 172064 | tf_op jit(solution)/shard_map/ppermute | solution.py:485
  228.2 5.5 %collective-permute-done.10.refs_4_ = f32[16,2688]{1,0:T(8,128)S(1)} collective-permute-done((f32[16,2688]{1,0:T(8,128)S(1)}, f32[16,2688]{1,0:T(8,128)S(1)}, u32[]{:S(2)}, u32[]{:S(2)}) %collective-permute-start.10) | collective-permute-done | bytes 172064 | tf_op jit(solution)/shard_map/ppermute | solution.py:485
  234.3 2.4 collective-permute-done.11.refs_5_
  243.9 5.1 %collective-permute-done.17.refs_12_ = f32[16,2688]{1,0:T(8,128)S(1)} collective-permute-done((f32[16,2688]{1,0:T(8,128)S(1)}, f32[16,2688]{1,0:T(8,128)S(1)}, u32[]{:S(2)}, u32[]{:S(2)}) %collective-permute-start.17) | collective-permute-done | bytes 172064 | tf_op jit(solution)/shard_map/ppermute | solution.py:485
  250.9 4.4 %collective-permute-done.19.refs_14_ = f32[16,2688]{1,0:T(8,128)S(1)} collective-permute-done((f32[16,2688]{1,0:T(8,128)S(1)}, f32[16,2688]{1,0:T(8,128)S(1)}, u32[]{:S(2)}, u32[]{:S(2)}) %collective-permute-start.19) | collective-permute-done | bytes 172064 | tf_op jit(solution)/shard_map/ppermute | solution.py:485
  255.3 3.7 %collective-permute-done.20.refs_15_ = f32[16,2688]{1,0:T(8,128)S(1)} collective-permute-done((f32[16,2688]{1,0:T(8,128)S(1)}, f32[16,2688]{1,0:T(8,128)S(1)}, u32[]{:S(2)}, u32[]{:S(2)}) %collective-permute-start.20) | collective-permute-done | bytes 172064 | tf_op jit(solution)/shard_map/ppermute | solution.py:485
  259.7 12.5 %gram.1 = f32[16,40,320]{2,1,0:T(8,128)} custom-call(s32[3]{0:T(128)} %pad_add_fusion.info.refs_0_, f32[16,2688]{1,0:T(8,128)} %get-tuple-element.73.refs_0_, f32[16,2688]{1,0:T(8,128)} %copy-done.15, f32[16,2688]{1,0:T(8,128)} %copy-done.18, f32[16,2688]{1,0:T(8,128)} %copy-done.19, f32[16,2688]{1,0:T(8,128)} %copy-done.21, f32[16,2688]{1,0:T(8,128)} %copy-done.23, ...), custom_call_target="tpu_custom_call" | custom-call | flops 4000000000 | bytes 8000000 | tf_op jit(solution)/shard_map/gram/pallas_call | solution.py:462
  272.1 23.9 %all_to_all.46 = f32[16,40,320]{2,1,0:T(8,128)S(1)} all-to-all(f32[16,40,320]{2,1,0:T(8,128)} %gram.1), channel_id=1, replica_groups=mesh['dom'=16,'band'=8] {'dom'}, dimensions={0} | all-to-all | bytes 1638400 | tf_op jit(solution)/shard_map/all_to_all | solution.py:521
  297.1 3.3 %all-to-all-start.8 = ((f32[8,1,1600]{2,1,0:T(1,128)}), f32[8,1,1600]{2,1,0:T(1,128)S(1)}, u32[]{:S(2)}, u32[]{:S(2)}) async-start(f32[8,1,1600]{2,1,0:T(1,128)} %reshape.76), calls=%async_computation.8 | async-start | bytes 106496 | tf_op jit(solution)/shard_map/all_to_all | solution.py:523
  300.4 2.4 unpack_rest.1
  302.8 3.1 %all-to-all-done.8 = f32[8,1,1600]{2,1,0:T(1,128)S(1)} async-done(((f32[8,1,1600]{2,1,0:T(1,128)}), f32[8,1,1600]{2,1,0:T(1,128)S(1)}, u32[]{:S(2)}, u32[]{:S(2)}) %all-to-all-start.8) | async-done | bytes 51232 | tf_op jit(solution)/shard_map/all_to_all | solution.py:523
  (124 shorter events, 33.1 us)
Async XLA Ops:
  39.3 23.8 %all-to-all-start.1 = ((f32[16,168,128]{2,1,0:T(8,128)}), f32[16,168,128]{2,1,0:T(8,128)S(1)}, u32[]{:S(2)}, u32[]{:S(2)}) async-start(f32[16,168,128]{2,1,0:T(8,128)} %bitcast.36), calls=%async_computation.1 | async-start | bytes 2752512 | tf_op jit(solution)/shard_map/all_to_all | solution.py:478
  43.1 5.2 %collective-permute-start = (f32[384,128]{1,0:T(8,128)S(1)}, f32[384,128]{1,0:T(8,128)S(1)}, u32[]{:S(2)}, u32[]{:S(2)}) collective-permute-start(f32[384,128]{1,0:T(8,128)S(1)} %bitcast.40), channel_id=1, source_target_pairs={{0,1},{1,0},{2,3},{3,2},{4,5},{5,4},{6,7},{7,6},{8,9},{9,8},{10,11... | collective-permute-start | bytes 589832 | tf_op jit(solution)/shard_map/ppermute | solution.py:485
  43.2 8.1 %collective-permute-start.1 = (f32[384,128]{1,0:T(8,128)S(1)}, f32[384,128]{1,0:T(8,128)S(1)}, u32[]{:S(2)}, u32[]{:S(2)}) collective-permute-start(f32[384,128]{1,0:T(8,128)S(1)} %bitcast.41), channel_id=1, source_target_pairs={{0,2},{1,3},{2,0},{3,1},{4,6},{5,7},{6,4},{7,5},{8,10},{9,11},{10,... | collective-permute-start | bytes 589832 | tf_op jit(solution)/shard_map/ppermute | solution.py:485
  44.8 23.1 %collective-permute-start.2 = (f32[384,128]{1,0:T(8,128)S(1)}, f32[384,128]{1,0:T(8,128)S(1)}, u32[]{:S(2)}, u32[]{:S(2)}) collective-permute-start(f32[384,128]{1,0:T(8,128)S(1)} %bitcast.42), channel_id=1, source_target_pairs={{0,3},{1,2},{2,1},{3,0},{4,7},{5,6},{6,5},{7,4},{8,11},{9,10},{10,... | collective-permute-start | bytes 589832 | tf_op jit(solution)/shard_map/ppermute | solution.py:485
  45.0 23.0 %collective-permute-start.3 = (f32[384,128]{1,0:T(8,128)S(1)}, f32[384,128]{1,0:T(8,128)}, u32[]{:S(2)}, u32[]{:S(2)}) collective-permute-start(f32[384,128]{1,0:T(8,128)S(1)} %bitcast.43), channel_id=1, source_target_pairs={{0,4},{1,5},{2,6},{3,7},{4,0},{5,1},{6,2},{7,3},{8,12},{9,13},{10,... | collective-permute-start | bytes 589832 | tf_op jit(solution)/shard_map/ppermute | solution.py:485
  48.2 19.8 %collective-permute-start.4 = (f32[384,128]{1,0:T(8,128)S(1)}, f32[384,128]{1,0:T(8,128)}, u32[]{:S(2)}, u32[]{:S(2)}) collective-permute-start(f32[384,128]{1,0:T(8,128)S(1)} %bitcast.44), channel_id=1, source_target_pairs={{0,5},{1,4},{2,7},{3,6},{4,1},{5,0},{6,3},{7,2},{8,13},{9,12},{10,... | collective-permute-start | bytes 589832 | tf_op jit(solution)/shard_map/ppermute | solution.py:485
  48.3 19.8 %collective-permute-start.5 = (f32[384,128]{1,0:T(8,128)S(1)}, f32[384,128]{1,0:T(8,128)}, u32[]{:S(2)}, u32[]{:S(2)}) collective-permute-start(f32[384,128]{1,0:T(8,128)S(1)} %bitcast.45), channel_id=1, source_target_pairs={{0,6},{1,7},{2,4},{3,5},{4,2},{5,3},{6,0},{7,1},{8,14},{9,15},{10,... | collective-permute-start | bytes 589832 | tf_op jit(solution)/shard_map/ppermute | solution.py:485
  51.3 17.7 %collective-permute-start.6 = (f32[384,128]{1,0:T(8,128)S(1)}, f32[384,128]{1,0:T(8,128)}, u32[]{:S(2)}, u32[]{:S(2)}) collective-permute-start(f32[384,128]{1,0:T(8,128)S(1)} %bitcast.46), channel_id=1, source_target_pairs={{0,7},{1,6},{2,5},{3,4},{4,3},{5,2},{6,1},{7,0},{8,15},{9,14},{10,... | collective-permute-start | bytes 589832 | tf_op jit(solution)/shard_map/ppermute | solution.py:485
  64.3 24.6 %all-to-all-start.2 = ((f32[16,168,128]{2,1,0:T(8,128)}), f32[16,168,128]{2,1,0:T(8,128)S(1)}, u32[]{:S(2)}, u32[]{:S(2)}) async-start(f32[16,168,128]{2,1,0:T(8,128)} %bitcast.34), calls=%async_computation.2 | async-start | bytes 2752512 | tf_op jit(solution)/shard_map/all_to_all | solution.py:478
  90.0 30.0 %all-to-all-start.3 = ((f32[16,168,128]{2,1,0:T(8,128)}), f32[16,168,128]{2,1,0:T(8,128)S(1)}, u32[]{:S(2)}, u32[]{:S(2)}) async-start(f32[16,168,128]{2,1,0:T(8,128)} %bitcast.37), calls=%async_computation.3 | async-start | bytes 2752512 | tf_op jit(solution)/shard_map/all_to_all | solution.py:478
  124.4 24.9 %all-to-all-start.4 = ((f32[16,168,128]{2,1,0:T(8,128)}), f32[16,168,128]{2,1,0:T(8,128)S(1)}, u32[]{:S(2)}, u32[]{:S(2)}) async-start(f32[16,168,128]{2,1,0:T(8,128)} %bitcast.13), calls=%async_computation.4 | async-start | bytes 2752512 | tf_op jit(solution)/shard_map/all_to_all | solution.py:478
  149.3 17.7 %all-to-all-start.5 = ((f32[16,96,128]{2,1,0:T(8,128)}), f32[16,96,128]{2,1,0:T(8,128)S(1)}, u32[]{:S(2)}, u32[]{:S(2)}) async-start(f32[16,96,128]{2,1,0:T(8,128)} %bitcast.38), calls=%async_computation.5 | async-start | bytes 1572864 | tf_op jit(solution)/shard_map/all_to_all | solution.py:478
  167.1 72.2 %copy-start.12 = (f32[16,2688]{1,0:T(8,128)S(1)}, f32[16,2688]{1,0:T(8,128)}, u32[]{:S(2)}) copy-start(f32[16,2688]{1,0:T(8,128)} %get-tuple-element.86) | copy-start | bytes 516100
  167.2 73.0 %copy-start.11 = (f32[16,2688]{1,0:T(8,128)S(1)}, f32[16,2688]{1,0:T(8,128)}, u32[]{:S(2)}) copy-start(f32[16,2688]{1,0:T(8,128)} %get-tuple-element.87) | copy-start | bytes 516100
  167.2 75.0 %copy-start.10 = (f32[16,2688]{1,0:T(8,128)S(1)}, f32[16,2688]{1,0:T(8,128)}, u32[]{:S(2)}) copy-start(f32[16,2688]{1,0:T(8,128)} %get-tuple-element.88) | copy-start | bytes 516100
  167.9 91.1 %all-to-all-start.6 = ((f32[128,64,128]{2,1,0:T(8,128)}), f32[128,64,128]{2,1,0:T(8,128)}, u32[]{:S(2)}, u32[]{:S(2)}) async-start(f32[128,64,128]{2,1,0:T(8,128)} %bitcast.24), calls=%async_computation.6 | async-start | bytes 8388608 | tf_op jit(solution)/shard_map/all_to_all | solution.py:478
  174.8 5.2 %collective-permute-start.7 = (f32[16,2688]{1,0:T(8,128)S(1)}, f32[16,2688]{1,0:T(8,128)S(1)}, u32[]{:S(2)}, u32[]{:S(2)}) collective-permute-start(f32[16,2688]{1,0:T(8,128)S(1)} %copy-done.31), channel_id=1, source_target_pairs={{0,1},{1,0},{2,3},{3,2},{4,5},{5,4},{6,7},{7,6},{8,9},{9,8},{10,11... | collective-permute-start | bytes 516104 | tf_op jit(solution)/shard_map/ppermute | solution.py:485
  174.9 49.8 %collective-permute-start.8 = (f32[16,2688]{1,0:T(8,128)S(1)}, f32[16,2688]{1,0:T(8,128)S(1)}, u32[]{:S(2)}, u32[]{:S(2)}) collective-permute-start(f32[16,2688]{1,0:T(8,128)S(1)} %copy-done.29), channel_id=1, source_target_pairs={{0,2},{1,3},{2,0},{3,1},{4,6},{5,7},{6,4},{7,5},{8,10},{9,11},{10,... | collective-permute-start | bytes 516104 | tf_op jit(solution)/shard_map/ppermute | solution.py:485
  175.8 51.5 %collective-permute-start.9 = (f32[16,2688]{1,0:T(8,128)S(1)}, f32[16,2688]{1,0:T(8,128)S(1)}, u32[]{:S(2)}, u32[]{:S(2)}) collective-permute-start(f32[16,2688]{1,0:T(8,128)S(1)} %copy-done.27), channel_id=1, source_target_pairs={{0,3},{1,2},{2,1},{3,0},{4,7},{5,6},{6,5},{7,4},{8,11},{9,10},{10,... | collective-permute-start | bytes 516104 | tf_op jit(solution)/shard_map/ppermute | solution.py:485
  176.7 57.0 %collective-permute-start.10 = (f32[16,2688]{1,0:T(8,128)S(1)}, f32[16,2688]{1,0:T(8,128)S(1)}, u32[]{:S(2)}, u32[]{:S(2)}) collective-permute-start(f32[16,2688]{1,0:T(8,128)S(1)} %copy-done.25), channel_id=1, source_target_pairs={{0,4},{1,5},{2,6},{3,7},{4,0},{5,1},{6,2},{7,3},{8,12},{9,13},{10,... | collective-permute-start | bytes 516104 | tf_op jit(solution)/shard_map/ppermute | solution.py:485
  179.1 57.5 %collective-permute-start.11 = (f32[16,2688]{1,0:T(8,128)S(1)}, f32[16,2688]{1,0:T(8,128)S(1)}, u32[]{:S(2)}, u32[]{:S(2)}) collective-permute-start(f32[16,2688]{1,0:T(8,128)S(1)} %copy-done.22), channel_id=1, source_target_pairs={{0,5},{1,4},{2,7},{3,6},{4,1},{5,0},{6,3},{7,2},{8,13},{9,12},{10,... | collective-permute-start | bytes 516104 | tf_op jit(solution)/shard_map/ppermute | solution.py:485
  179.9 79.1 %copy-start.15 = (f32[16,2688]{1,0:T(8,128)}, f32[16,2688]{1,0:T(8,128)S(1)}, u32[]{:S(2)}) copy-start(f32[16,2688]{1,0:T(8,128)S(1)} %collective-permute-done.7.refs_1_) | copy-start | bytes 516100
  179.9 57.4 %collective-permute-start.12 = (f32[16,2688]{1,0:T(8,128)S(1)}, f32[16,2688]{1,0:T(8,128)S(1)}, u32[]{:S(2)}, u32[]{:S(2)}) collective-permute-start(f32[16,2688]{1,0:T(8,128)S(1)} %copy-done.17), channel_id=1, source_target_pairs={{0,6},{1,7},{2,4},{3,5},{4,2},{5,3},{6,0},{7,1},{8,14},{9,15},{10,... | collective-permute-start | bytes 516104 | tf_op jit(solution)/shard_map/ppermute | solution.py:485
  224.7 14.7 %collective-permute-start.13 = (f32[16,2688]{1,0:T(8,128)S(1)}, f32[16,2688]{1,0:T(8,128)S(1)}, u32[]{:S(2)}, u32[]{:S(2)}) collective-permute-start(f32[16,2688]{1,0:T(8,128)S(1)} %copy-done.13), channel_id=1, source_target_pairs={{0,7},{1,6},{2,5},{3,4},{4,3},{5,2},{6,1},{7,0},{8,15},{9,14},{10,... | collective-permute-start | bytes 516104 | tf_op jit(solution)/shard_map/ppermute | solution.py:485
  227.4 12.8 %collective-permute-start.14 = (f32[16,2688]{1,0:T(8,128)S(1)}, f32[16,2688]{1,0:T(8,128)S(1)}, u32[]{:S(2)}, u32[]{:S(2)}) collective-permute-start(f32[16,2688]{1,0:T(8,128)S(1)} %copy-done.24), channel_id=1, source_target_pairs={{0,1},{1,0},{2,3},{3,2},{4,5},{5,4},{6,7},{7,6},{8,9},{9,8},{10,11... | collective-permute-start | bytes 516104 | tf_op jit(solution)/shard_map/ppermute | solution.py:485
  233.7 8.5 %collective-permute-start.15 = (f32[16,2688]{1,0:T(8,128)S(1)}, f32[16,2688]{1,0:T(8,128)S(1)}, u32[]{:S(2)}, u32[]{:S(2)}) collective-permute-start(f32[16,2688]{1,0:T(8,128)S(1)} %copy-done.20), channel_id=1, source_target_pairs={{0,2},{1,3},{2,0},{3,1},{4,6},{5,7},{6,4},{7,5},{8,10},{9,11},{10,... | collective-permute-start | bytes 516104 | tf_op jit(solution)/shard_map/ppermute | solution.py:485
  236.6 7.2 %collective-permute-start.16 = (f32[16,2688]{1,0:T(8,128)S(1)}, f32[16,2688]{1,0:T(8,128)S(1)}, u32[]{:S(2)}, u32[]{:S(2)}) collective-permute-start(f32[16,2688]{1,0:T(8,128)S(1)} %copy-done.16), channel_id=1, source_target_pairs={{0,3},{1,2},{2,1},{3,0},{4,7},{5,6},{6,5},{7,4},{8,11},{9,10},{10,... | collective-permute-start | bytes 516104 | tf_op jit(solution)/shard_map/ppermute | solution.py:485
  237.3 11.6 %collective-permute-start.17 = (f32[16,2688]{1,0:T(8,128)S(1)}, f32[16,2688]{1,0:T(8,128)S(1)}, u32[]{:S(2)}, u32[]{:S(2)}) collective-permute-start(f32[16,2688]{1,0:T(8,128)S(1)} %copy-done.14), channel_id=1, source_target_pairs={{0,4},{1,5},{2,6},{3,7},{4,0},{5,1},{6,2},{7,3},{8,12},{9,13},{10,... | collective-permute-start | bytes 516104 | tf_op jit(solution)/shard_map/ppermute | solution.py:485
  239.4 11.6 %collective-permute-start.18 = (f32[16,2688]{1,0:T(8,128)S(1)}, f32[16,2688]{1,0:T(8,128)S(1)}, u32[]{:S(2)}, u32[]{:S(2)}) collective-permute-start(f32[16,2688]{1,0:T(8,128)S(1)} %copy-done.12), channel_id=1, source_target_pairs={{0,5},{1,4},{2,7},{3,6},{4,1},{5,0},{6,3},{7,2},{8,13},{9,12},{10,... | collective-permute-start | bytes 516104 | tf_op jit(solution)/shard_map/ppermute | solution.py:485
  240.2 15.1 %collective-permute-start.19 = (f32[16,2688]{1,0:T(8,128)S(1)}, f32[16,2688]{1,0:T(8,128)S(1)}, u32[]{:S(2)}, u32[]{:S(2)}) collective-permute-start(f32[16,2688]{1,0:T(8,128)S(1)} %copy-done.11), channel_id=1, source_target_pairs={{0,6},{1,7},{2,4},{3,5},{4,2},{5,3},{6,0},{7,1},{8,14},{9,15},{10,... | collective-permute-start | bytes 516104 | tf_op jit(solution)/shard_map/ppermute | solution.py:485
  242.2 16.8 %collective-permute-start.20 = (f32[16,2688]{1,0:T(8,128)S(1)}, f32[16,2688]{1,0:T(8,128)S(1)}, u32[]{:S(2)}, u32[]{:S(2)}) collective-permute-start(f32[16,2688]{1,0:T(8,128)S(1)} %copy-done.10), channel_id=1, source_target_pairs={{0,7},{1,6},{2,5},{3,4},{4,3},{5,2},{6,1},{7,0},{8,15},{9,14},{10,... | collective-permute-start | bytes 516104 | tf_op jit(solution)/shard_map/ppermute | solution.py:485
  297.1 8.8 %all-to-all-start.8 = ((f32[8,1,1600]{2,1,0:T(1,128)}), f32[8,1,1600]{2,1,0:T(1,128)S(1)}, u32[]{:S(2)}, u32[]{:S(2)}) async-start(f32[8,1,1600]{2,1,0:T(1,128)} %reshape.76), calls=%async_computation.8 | async-start | bytes 106496 | tf_op jit(solution)/shard_map/all_to_all | solution.py:523
  (34 other events, 671.7 us)
